TPU v7x, 256 devices: a whole 4x4x8 slice. The times are simulated.
256 devices in a mesh: sec: 2 (over x_hi), tile: 128 (over z, y, x_lo, core).
Axes of the slice: x: 4 (x_hi: 2, x_lo: 2; x = x_hi * 2 + x_lo), y: 4, z: 8, core: 2. Of those that a mesh axis runs over, the one named last changes fastest.
Arguments:
- load_field: float32 [3, 512, 256, 128], P(None, 'tile', 'sec'), may hold values from -6 to 6
- iterate: float32 [3, 512, 256, 128], P(None, 'tile', 'sec'), may hold values from -3 to 3
- phase_label: int32 [512, 256, 128], P('tile', 'sec'), may hold values from 0 to 3
- damage: int32 [512, 256, 128], P('tile', 'sec'), may hold values from 0 to 3
Outputs:
- correction: float32 [3, 512, 256, 128], P(None, 'tile', 'sec')
All inputs are finite; a program needn't handle non-finite values.
Results may differ from a plain program's by a relative error of at most 0.0001.
Values sent between devices are 32-bit elements; how exact they have to be, the bound alone decides.
A program may use at most 64 MiB of HBM per device.

v0:
```python
import jax
import jax.numpy as jnp
from jax import lax
from jax.sharding import PartitionSpec as P

shear_table = (1.0, 0.6, 1.8, 0.35)
bulk_table = (1.2, 0.9, 2.5, 0.5)
damage_step = 0.25
damage_floor = 0.01
relaxation = 2.0 / 3.0


def with_halo(shard, sides, width):
    for axis, dim in sides:
        size, length = (lax.axis_size(axis), shard.shape[dim])
        up = [(i, (i + 1) % size) for i in range(size - 1)]
        down = [(j, i) for i, j in up]
        last = lax.slice_in_dim(shard, length - width, length, axis=dim)
        first = lax.slice_in_dim(shard, 0, width, axis=dim)
        before = lax.ppermute(last, axis, up)
        after = lax.ppermute(first, axis, down)
        shard = jnp.concatenate([before, shard, after], axis=dim)
    return shard


def material(phase_label, damage):
    shear = jnp.zeros(phase_label.shape, jnp.float32)
    bulk = jnp.zeros(phase_label.shape, jnp.float32)
    for label in range(len(shear_table)):
        hit = phase_label == label
        shear = shear + jnp.where(hit, shear_table[label], 0.0)
        bulk = bulk + jnp.where(hit, bulk_table[label], 0.0)
    soft = 1.0 - damage_step * damage.astype(jnp.float32)
    degrade = soft * soft + damage_floor
    return (shear * degrade, bulk * degrade)


def depth_shift(array, offset):
    if offset == 1:
        return array
    last = array.ndim - 1
    place = lax.broadcasted_iota(jnp.int32, array.shape, last)
    if offset == 0:
        return jnp.where(place == 0, 0.0, jnp.roll(array, 1, axis=last))
    return jnp.where(place == array.shape[last] - 1, 0.0, jnp.roll(array, -1, axis=last))


def neighbour(array, direction, offset):
    leading = array.ndim - 3
    selector = (
        [slice(None)] * leading
        + [slice(1, extent - 1) for extent in array.shape[leading : leading + 2]]
        + [slice(None)]
    )
    if direction < 2:
        extent = array.shape[leading + direction]
        selector[leading + direction] = slice(offset, offset + extent - 2)
        return array[tuple(selector)]
    return depth_shift(array[tuple(selector)], offset)


def face_weights(padded_shear, padded_bulk):
    result = []
    for direction in range(3):
        unit_row = jnp.array(
            [1.0 if comp_index == direction else 0.0 for comp_index in range(3)], jnp.float32
        )
        for offset in (0, 2):
            face_shear = 0.5 * (
                neighbour(padded_shear, direction, 1) + neighbour(padded_shear, direction, offset)
            )
            face_bulk = 0.5 * (
                neighbour(padded_bulk, direction, 1) + neighbour(padded_bulk, direction, offset)
            )
            result.append(
                face_shear[None] + unit_row[:, None, None, None] * (face_bulk + face_shear)[None]
            )
    return result


def operate(padded, weights):
    running = None
    counter = 0
    for direction in range(3):
        for offset in (0, 2):
            term = weights[counter] * (
                neighbour(padded, direction, 1) - neighbour(padded, direction, offset)
            )
            running = term if running is None else running + term
            counter += 1
    return running


def diagonal_of(weights):
    running = weights[0]
    for face_weight in weights[1:]:
        running = running + face_weight
    return running


def pair_table(depth, pick):
    fine_pos = jnp.arange(depth, dtype=jnp.int32)[:, None]
    coarse_pos = jnp.arange(depth // 2, dtype=jnp.int32)[None, :]
    if pick < 0:
        hit = fine_pos // 2 == coarse_pos
    else:
        hit = fine_pos == 2 * coarse_pos + pick
    return hit.astype(jnp.float32)


def along_depth(field, table):
    return jnp.einsum("cxyk,kj->cxyj", field, table, precision=lax.Precision.HIGHEST)


def coarsen(weights):
    result = []
    counter = 0
    for direction in range(3):
        for child_pos in (0, 1):
            face_weight = weights[counter]
            comps, rows, cols, depth = face_weight.shape
            blocks = face_weight.reshape(comps, rows // 2, 2, cols // 2, 2, depth)
            if direction == 0:
                planar = blocks[:, :, child_pos].sum(axis=3)
            elif direction == 1:
                planar = blocks[:, :, :, :, child_pos].sum(axis=2)
            else:
                planar = blocks.sum(axis=(2, 4))
            table = pair_table(depth, child_pos if direction == 2 else -1)
            result.append(along_depth(planar, table))
            counter += 1
    return result


def restrict(field):
    comps, rows, cols, depth = field.shape
    planar = field.reshape(comps, rows // 2, 2, cols // 2, 2, depth).sum(axis=(2, 4))
    return along_depth(planar, pair_table(depth, -1))


def prolong(field):
    spread = jnp.repeat(jnp.repeat(field, 2, axis=1), 2, axis=2)
    table = pair_table(2 * field.shape[3], -1)
    return jnp.einsum("cxyj,kj->cxyk", spread, table, precision=lax.Precision.HIGHEST)


def begin_sweep(residual, weights):
    diagonal = diagonal_of(weights)
    return (relaxation * residual / diagonal, diagonal)


def end_sweep(first_sweep, extended, residual, weights, diagonal):
    return first_sweep + relaxation * (residual - operate(extended, weights)) / diagonal


def middle_padder(field):
    return with_halo(field, (("sec", 2), ("tile", 1)), 1)


def bottom_padder(field):
    return with_halo(field, (("sec", 2), ("tile", 1)), 1)


def fine_padder(field):
    return with_halo(field, (("sec", 2), ("tile", 1)), 1)


def per_device(load_field, iterate, phase_label, damage):
    shear, bulk = material(phase_label, damage)
    stacked = jnp.concatenate([shear[None], bulk[None], iterate], axis=0)
    padded = with_halo(stacked, (("sec", 2), ("tile", 1)), 1)
    weights = face_weights(padded[0], padded[1])
    residual = load_field - operate(padded[2:5], weights)
    fine_first, fine_diagonal = begin_sweep(residual, weights)
    fine_corr = None
    weights_two = coarsen(weights)
    residual_two = restrict(residual)
    middle_first, middle_diagonal = begin_sweep(residual_two, weights_two)
    weights_three = coarsen(weights_two)
    residual_three = restrict(residual_two)
    bottom_first, bottom_diagonal = begin_sweep(residual_three, weights_three)
    fine_ext = fine_padder(fine_first)
    middle_ext = middle_padder(middle_first)
    bottom_ext = bottom_padder(bottom_first)
    fine_corr = end_sweep(fine_first, fine_ext, residual, weights, fine_diagonal)
    middle_corr = end_sweep(middle_first, middle_ext, residual_two, weights_two, middle_diagonal)
    bottom_corr = end_sweep(
        bottom_first, bottom_ext, residual_three, weights_three, bottom_diagonal
    )
    return fine_corr + prolong(middle_corr + prolong(bottom_corr))


def solution(mesh):
    in_specs = (
        P(None, "tile", "sec", None),
        P(None, "tile", "sec", None),
        P("tile", "sec", None),
        P("tile", "sec", None),
    )
    out_specs = P(None, "tile", "sec", None)
    return jax.shard_map(
        per_device, mesh=mesh, in_specs=in_specs, out_specs=out_specs, check_vma=False
    )
```

profile of v0, /device:TPU:127, one launch (start us, length us, event | category | flops | bytes accessed | tf_op | source)
XLA Modules:
  0.0 134.5 jit_solution(12680036122273143121)
XLA Ops:
  0.0 1.4 %multiply_bitcast_fusion.1 = (f32[1,4,128,128]{3,2,1,0:T(8,128)S(1)}, pred[4,128,128]{2,1,0:T(8,128)(4,1)S(1)}, pred[4,128,128]{2,1,0:T(8,128)(4,1)S(1)}, pred[4...) fusion(s32[4,128,128]{2,1,0:T(8,128)} %param.10, s32[4,128,128]{2,1,0:T(8,128)} %param.9), kind=kLoop, calls=%fused_computation.131 | loop fusion | flops 1114112 | bytes 1048576 | tf_op jit(solution)/shard_map/broadcast_in_dim | solution.py:170
  1.6 1.3 collective-permute-start
  2.9 5.5 %collective-permute-start.1 = (f32[5,4,1,128]{3,2,1,0:T(1,128)S(1)}, f32[5,4,1,128]{3,2,1,0:T(1,128)S(1)}, u32[]{:S(2)}, u32[]{:S(2)}) collective-permute-start(f32[5,4,1,128]{3,2,1,0:T(1,128)S(1)} %get-tuple-element.35), channel_id=1, source_target_pairs={{128,0},{129,1},{130,2},{131,3},{132,4},{133,5},{134,6},{135,7},{1... | collective-permute-start | bytes 30728 | tf_op jit(solution)/shard_map/ppermute | solution.py:21
  8.5 1.4 %fusion.173 = (f32[3,4,128,1]{3,2,1,0:T(8,128)}, f32[3,4,128,1]{3,2,1,0:T(8,128)}) fusion(f32[3,4,128,128]{3,2,1,0:T(8,128)S(1)} %copy-done), kind=kLoop, calls=%fused_computation.282 | loop fusion | bytes 24576 | tf_op jit(solution)/shard_map/jit(_roll_static)/slice | solution.py:44
  12.1 5.8 %collective-permute-start.2 = (f32[5,1,130,128]{3,2,1,0:T(8,128)S(1)}, f32[5,1,130,128]{3,2,1,0:T(8,128)S(1)}, u32[]{:S(2)}, u32[]{:S(2)}) collective-permute-start(f32[5,1,130,128]{3,2,1,0:T(8,128)S(1)} %get-tuple-element.32), channel_id=1, source_target_pairs={{0,1},{1,2},{2,3},{3,4},{4,5},{5,6},{6,7},{7,8},{8,9},{9,10},{10,1... | collective-permute-start | bytes 998408 | tf_op jit(solution)/shard_map/ppermute | solution.py:20
  17.9 1.9 %collective-permute-start.3 = (f32[5,1,130,128]{3,2,1,0:T(8,128)S(1)}, f32[5,1,130,128]{3,2,1,0:T(8,128)S(1)}, u32[]{:S(2)}, u32[]{:S(2)}) collective-permute-start(f32[5,1,130,128]{3,2,1,0:T(8,128)S(1)} %get-tuple-element.33), channel_id=1, source_target_pairs={{1,0},{2,1},{3,2},{4,3},{5,4},{6,5},{7,6},{8,7},{9,8},{10,9},{11,1... | collective-permute-start | bytes 998408 | tf_op jit(solution)/shard_map/ppermute | solution.py:21
  20.4 1.4 %fusion.174 = (f32[3,4,128,127]{3,2,1,0:T(8,128)}, f32[3,4,128,127]{3,2,1,0:T(8,128)}) fusion(f32[3,4,128,128]{3,2,1,0:T(8,128)S(1)} %copy-done), kind=kLoop, calls=%fused_computation.283 | loop fusion | bytes 3121152 | tf_op jit(solution)/shard_map/jit(_roll_static)/slice | solution.py:44
  22.1 8.6 %collective-permute-done.3 = f32[5,1,130,128]{3,2,1,0:T(8,128)S(1)} collective-permute-done((f32[5,1,130,128]{3,2,1,0:T(8,128)S(1)}, f32[5,1,130,128]{3,2,1,0:T(8,128)S(1)}, u32[]{:S(2)}, u32[]{:S(2)}) %collective-permute-start.3) | collective-permute-done | bytes 332832 | tf_op jit(solution)/shard_map/ppermute | solution.py:21
  45.7 4.7 %fusion.39 = (f32[3,4,128,128]{3,2,1,0:T(8,128)S(1)}, f32[3,4,128,128]{3,2,1,0:T(8,128)}) fusion(f32[4,128,128]{2,1,0:T(8,128)S(1)} %get-tuple-element.36, f32[4,128,128]{2,1,0:T(8,128)S(1)} %get-tuple-element.37, f32[4,128,128]{2,1,0:T(8,128)S(1)} %get-tuple-element.42, f32[3]{0:T(128)S(1)} %copy-done.47, f32[4,128,128]{2,1,0:T(8,128)S(1)} %get-tuple-element.43, ...), kind=kLoop, calls=%fused_computation.72 | loop fusion | flops 11206656 | bytes 9074980 | tf_op jit(solution)/shard_map/div | solution.py:149
  50.4 2.4 %reduce_sum.147 = f32[3,2,64,128]{3,2,1,0:T(8,128)} reduce(f32[3,2,2,64,2,128]{5,4,3,2,1,0:T(2,128)} %bitcast.146, f32[]{:T(128)} %constant.83.clone.1), dimensions={2,4}, to_apply=%region_0.1 | reduce | flops 147456 | bytes 983044 | tf_op jit(solution)/shard_map/reduce_sum | solution.py:137
  55.7 1.8 %fusion.179 = (f32[3,64,64]{1,2,0:T(8,128)}, f32[3,2,64,64]{2,3,1,0:T(8,128)S(1)}, f32[3,64,64]{1,2,0:T(8,128)}, f32[3,64,64]{1,2,0:T(8,128)S(1)}, f32[3,2,64,64]{2,3,1,0:T(8,128)}) fusion(f32[3,2,64,64]{2,3,1,0:T(8,128)S(1)} %fusion.125, f32[3,2,64,64]{2,3,1,0:T(8,128)S(1)} %fusion.122, f32[3,2,64,64]{2,3,1,0:T(8,128)S(1)} %copy-done.19, ...), kind=kOutput, calls=%fused_computation.288 | convolution fusion | flops 37965824 | bytes 1131008 | tf_op jit(solution)/shard_map/cxyk,kj->cxyj/dot_general | solution.py:112
  57.6 1.6 %copy.51 = f32[3,64,64]{2,1,0:T(8,128)} copy(f32[3,64,64]{1,2,0:T(8,128)} %get-tuple-element.64) | data formatting | bytes 98304 | tf_op jit(solution)/shard_map/reduce_sum | solution.py:137
  59.2 1.6 %reduce_sum.156 = f32[3,32,64]{2,1,0:T(8,128)} reduce(f32[3,32,2,64]{3,2,1,0:T(2,128)} %bitcast.154, f32[]{:T(128)} %constant.83.clone.1), dimensions={2}, to_apply=%region_8.9 | reduce | flops 6144 | bytes 73732 | tf_op jit(solution)/shard_map/reduce_sum | solution.py:137
  60.9 1.6 %copy.56 = f32[3,64,64]{2,1,0:T(8,128)} copy(f32[3,64,64]{1,2,0:T(8,128)} %get-tuple-element.66) | data formatting | bytes 98304 | tf_op jit(solution)/shard_map/reduce_sum | solution.py:128
  72.0 1.4 %fusion.170 = (f32[3,4,128,127]{3,2,1,0:T(8,128)}, f32[3,4,128,127]{3,2,1,0:T(8,128)}) fusion(f32[3,4,128,128]{3,2,1,0:T(8,128)S(1)} %get-tuple-element.11), kind=kLoop, calls=%fused_computation.279 | loop fusion | bytes 3121152 | tf_op jit(solution)/shard_map/jit(_roll_static)/slice | solution.py:45
  73.4 1.4 %fusion.171 = (f32[3,4,128,1]{3,2,1,0:T(8,128)}, f32[3,4,128,1]{3,2,1,0:T(8,128)}) fusion(f32[3,4,128,128]{3,2,1,0:T(8,128)S(1)} %get-tuple-element.11), kind=kLoop, calls=%fused_computation.280 | loop fusion | bytes 24576 | tf_op jit(solution)/shard_map/jit(_roll_static)/slice | solution.py:45
  74.8 1.3 collective-permute-start.12
  76.1 1.3 collective-permute-start.4
  77.4 5.5 %collective-permute-start.13 = (f32[3,1,1,32]{2,3,0,1:T(8,128)S(1)}, f32[3,1,1,32]{2,3,0,1:T(8,128)S(1)}, u32[]{:S(2)}, u32[]{:S(2)}) collective-permute-start(f32[3,1,1,32]{2,3,0,1:T(8,128)S(1)} %get-tuple-element.77), channel_id=1, source_target_pairs={{128,0},{129,1},{130,2},{131,3},{132,4},{133,5},{134,6},{135,7},{1... | collective-permute-start | bytes 1160 | tf_op jit(solution)/shard_map/ppermute | solution.py:21
  82.9 1.3 collective-permute-start.5
  84.2 1.3 collective-permute-start.8
  85.5 5.5 %collective-permute-start.9 = (f32[3,2,1,64]{2,3,1,0:T(8,128)S(1)}, f32[3,2,1,64]{2,3,1,0:T(8,128)S(1)}, u32[]{:S(2)}, u32[]{:S(2)}) collective-permute-start(f32[3,2,1,64]{2,3,1,0:T(8,128)S(1)} %get-tuple-element.71), channel_id=1, source_target_pairs={{128,0},{129,1},{130,2},{131,3},{132,4},{133,5},{134,6},{135,7},{1... | collective-permute-start | bytes 4616 | tf_op jit(solution)/shard_map/ppermute | solution.py:21
  91.1 2.9 %collective-permute-start.14 = (f32[3,1,34,32]{2,3,0,1:T(8,128)S(1)}, f32[3,1,34,32]{2,3,0,1:T(8,128)S(1)}, u32[]{:S(2)}, u32[]{:S(2)}) collective-permute-start(f32[3,1,34,32]{2,3,0,1:T(8,128)S(1)} %pad_maximum_fusion.49), channel_id=1, source_target_pairs={{0,1},{1,2},{2,3},{3,4},{4,5},{5,6},{6,7},{7,8},{8,9},{9,10},{10,1... | collective-permute-start | bytes 39176 | tf_op jit(solution)/shard_map/ppermute | solution.py:20
  94.0 1.9 %collective-permute-start.15 = (f32[3,1,34,32]{2,3,0,1:T(8,128)S(1)}, f32[3,1,34,32]{2,3,0,1:T(8,128)S(1)}, u32[]{:S(2)}, u32[]{:S(2)}) collective-permute-start(f32[3,1,34,32]{2,3,0,1:T(8,128)S(1)} %pad_maximum_fusion.49), channel_id=1, source_target_pairs={{1,0},{2,1},{3,2},{4,3},{5,4},{6,5},{7,6},{8,7},{9,8},{10,9},{11,1... | collective-permute-start | bytes 39176 | tf_op jit(solution)/shard_map/ppermute | solution.py:21
  97.3 7.8 %collective-permute-start.10 = (f32[3,1,66,64]{2,3,1,0:T(8,128)}, f32[3,1,66,64]{2,3,1,0:T(8,128)}, u32[]{:S(2)}, u32[]{:S(2)}) collective-permute-start(f32[3,1,66,64]{2,3,1,0:T(8,128)} %get-tuple-element.68), channel_id=1, source_target_pairs={{0,1},{1,2},{2,3},{3,4},{4,5},{5,6},{6,7},{7,8},{8,9},{9,10},{10,1... | collective-permute-start | bytes 152072 | tf_op jit(solution)/shard_map/ppermute | solution.py:20
  105.2 1.9 %collective-permute-start.11 = (f32[3,1,66,64]{2,3,1,0:T(8,128)}, f32[3,1,66,64]{2,3,1,0:T(8,128)}, u32[]{:S(2)}, u32[]{:S(2)}) collective-permute-start(f32[3,1,66,64]{2,3,1,0:T(8,128)} %get-tuple-element.69), channel_id=1, source_target_pairs={{1,0},{2,1},{3,2},{4,3},{5,4},{6,5},{7,6},{8,7},{9,8},{10,9},{11,1... | collective-permute-start | bytes 152072 | tf_op jit(solution)/shard_map/ppermute | solution.py:21
  108.0 7.9 %collective-permute-start.6 = (f32[3,1,130,128]{3,2,1,0:T(8,128)}, f32[3,1,130,128]{3,2,1,0:T(8,128)}, u32[]{:S(2)}, u32[]{:S(2)}) collective-permute-start(f32[3,1,130,128]{3,2,1,0:T(8,128)} %get-tuple-element.44), channel_id=1, source_target_pairs={{0,1},{1,2},{2,3},{3,4},{4,5},{5,6},{6,7},{7,8},{8,9},{9,10},{10,1... | collective-permute-start | bytes 599048 | tf_op jit(solution)/shard_map/ppermute | solution.py:20
  115.9 2.1 %collective-permute-start.7 = (f32[3,1,130,128]{3,2,1,0:T(8,128)}, f32[3,1,130,128]{3,2,1,0:T(8,128)}, u32[]{:S(2)}, u32[]{:S(2)}) collective-permute-start(f32[3,1,130,128]{3,2,1,0:T(8,128)} %get-tuple-element.45), channel_id=1, source_target_pairs={{1,0},{2,1},{3,2},{4,3},{5,4},{6,5},{7,6},{8,7},{9,8},{10,9},{11,1... | collective-permute-start | bytes 599048 | tf_op jit(solution)/shard_map/ppermute | solution.py:21
  119.7 2.8 %convolution_add_fusion.1 = f32[3,2,64,64]{2,3,1,0:T(8,128)} fusion(f32[3,2,64,64]{2,3,1,0:T(8,128)S(1)} %get-tuple-element.65, f32[3,2,64,64]{2,3,1,0:T(8,128)} %copy-done.30, f32[3,2,64,64]{2,3,1,0:T(8,128)} %copy-done.29, f32[3,2,64,64]{2,3,1,0:T(8,128)S(1)} %copy-done.19, f32[3,2,64,64]{2,3,1,0:T(8,128)} %fusion.113, ...), kind=kOutput, calls=%fused_computation.1 | convolution fusion | flops 10397696 | bytes 1210752 | tf_op jit(solution)/shard_map/cxyj,kj->cxyk/dot_general | solution.py:144
  122.5 1.8 %copy.61 = f32[3,2,64,64]{3,2,1,0:T(8,128)} copy(f32[3,2,64,64]{2,3,1,0:T(8,128)} %convolution_add_fusion.1) | data formatting | bytes 196608 | tf_op jit(solution)/shard_map/add | solution.py:190
  124.3 3.2 %collective-permute-done.7 = f32[3,1,130,128]{3,2,1,0:T(8,128)} collective-permute-done((f32[3,1,130,128]{3,2,1,0:T(8,128)}, f32[3,1,130,128]{3,2,1,0:T(8,128)}, u32[]{:S(2)}, u32[]{:S(2)}) %collective-permute-start.7) | collective-permute-done | bytes 199712 | tf_op jit(solution)/shard_map/ppermute | solution.py:21
  129.8 4.7 %convolution_add_fusion = f32[3,4,128,128]{3,2,1,0:T(8,128)} fusion(f32[3,4,128,64]{3,2,1,0:T(8,128)S(1)} %bitcast.147, f32[3,4,128,128]{3,2,1,0:T(8,128)S(1)} %get-tuple-element.11, f32[3,4,128,128]{3,2,1,0:T(8,128)S(1)} %copy-done.11, f32[3,4,1,128]{3,2,1,0:T(1,128)S(1)} %copy-done.40, f32[3,4,1,128]{3,2,1,0:T(1,128)S(1)} %copy-done.38, ...), kind=kOutput, calls=%fused_computation | convolution fusion | flops 161030144 | bytes 7883556 | tf_op jit(solution)/shard_map/cxyj,kj->cxyk/dot_general | solution.py:144
  (222 shorter events, 36.1 us)
Async XLA Ops:
  1.4 29.4 %copy-start.13 = (f32[1,4,128,128]{3,2,1,0:T(8,128)}, f32[1,4,128,128]{3,2,1,0:T(8,128)S(1)}, u32[]{:S(2)}) copy-start(f32[1,4,128,128]{3,2,1,0:T(8,128)S(1)} %get-tuple-element.25) | copy-start | bytes 786436
  1.6 29.2 %copy-start.12 = (f32[1,4,128,128]{3,2,1,0:T(8,128)}, f32[1,4,128,128]{3,2,1,0:T(8,128)S(1)}, u32[]{:S(2)}) copy-start(f32[1,4,128,128]{3,2,1,0:T(8,128)S(1)} %multiply_bitcast_fusion) | copy-start | bytes 786436
  1.6 10.4 %collective-permute-start = (f32[5,4,1,128]{3,2,1,0:T(1,128)S(1)}, f32[5,4,1,128]{3,2,1,0:T(1,128)S(1)}, u32[]{:S(2)}, u32[]{:S(2)}) collective-permute-start(f32[5,4,1,128]{3,2,1,0:T(1,128)S(1)} %get-tuple-element.34), channel_id=1, source_target_pairs={{0,128},{1,129},{2,130},{3,131},{4,132},{5,133},{6,134},{7,135},{8... | collective-permute-start | bytes 30728 | tf_op jit(solution)/shard_map/ppermute | solution.py:20
  2.9 9.1 %collective-permute-start.1 = (f32[5,4,1,128]{3,2,1,0:T(1,128)S(1)}, f32[5,4,1,128]{3,2,1,0:T(1,128)S(1)}, u32[]{:S(2)}, u32[]{:S(2)}) collective-permute-start(f32[5,4,1,128]{3,2,1,0:T(1,128)S(1)} %get-tuple-element.35), channel_id=1, source_target_pairs={{128,0},{129,1},{130,2},{131,3},{132,4},{133,5},{134,6},{135,7},{1... | collective-permute-start | bytes 30728 | tf_op jit(solution)/shard_map/ppermute | solution.py:21
  8.4 36.6 %copy-start.51 = (pred[128]{0:T(512)(128)(4,1)}, pred[128]{0:T(512)(128)(4,1)S(1)}, u32[]{:S(2)}) copy-start(pred[128]{0:T(512)(128)(4,1)S(1)} %get-tuple-element.88) | copy-start | bytes 388
  8.4 36.6 %copy-start.53 = (pred[128]{0:T(512)(128)(4,1)}, pred[128]{0:T(512)(128)(4,1)S(1)}, u32[]{:S(2)}) copy-start(pred[128]{0:T(512)(128)(4,1)S(1)} %get-tuple-element.87) | copy-start | bytes 388
  9.9 45.2 %copy-start.41 = (s32[128]{0:T(128)}, s32[128]{0:T(128)S(1)}, u32[]{:S(2)}) copy-start(s32[128]{0:T(128)S(1)} %and_select_fusion.1) | copy-start | bytes 1540
  12.1 10.0 %collective-permute-start.2 = (f32[5,1,130,128]{3,2,1,0:T(8,128)S(1)}, f32[5,1,130,128]{3,2,1,0:T(8,128)S(1)}, u32[]{:S(2)}, u32[]{:S(2)}) collective-permute-start(f32[5,1,130,128]{3,2,1,0:T(8,128)S(1)} %get-tuple-element.32), channel_id=1, source_target_pairs={{0,1},{1,2},{2,3},{3,4},{4,5},{5,6},{6,7},{7,8},{8,9},{9,10},{10,1... | collective-permute-start | bytes 998408 | tf_op jit(solution)/shard_map/ppermute | solution.py:20
  17.9 12.8 %collective-permute-start.3 = (f32[5,1,130,128]{3,2,1,0:T(8,128)S(1)}, f32[5,1,130,128]{3,2,1,0:T(8,128)S(1)}, u32[]{:S(2)}, u32[]{:S(2)}) collective-permute-start(f32[5,1,130,128]{3,2,1,0:T(8,128)S(1)} %get-tuple-element.33), channel_id=1, source_target_pairs={{1,0},{2,1},{3,2},{4,3},{5,4},{6,5},{7,6},{8,7},{9,8},{10,9},{11,1... | collective-permute-start | bytes 998408 | tf_op jit(solution)/shard_map/ppermute | solution.py:21
  22.1 8.7 %copy-start.22 = (f32[5,1,130,128]{3,2,1,0:T(8,128)}, f32[5,1,130,128]{3,2,1,0:T(8,128)S(1)}, u32[]{:S(2)}) copy-start(f32[5,1,130,128]{3,2,1,0:T(8,128)S(1)} %collective-permute-done.2) | copy-start | bytes 998404
  32.3 3.4 %copy-start.5 = (f32[4,128,128]{2,1,0:T(8,128)}, f32[4,128,128]{2,1,0:T(8,128)S(1)}, u32[]{:S(2)}) copy-start(f32[4,128,128]{2,1,0:T(8,128)S(1)} %get-tuple-element.39) | copy-start | bytes 786436
  32.3 3.6 %copy-start.3 = (f32[4,128,128]{2,1,0:T(8,128)}, f32[4,128,128]{2,1,0:T(8,128)S(1)}, u32[]{:S(2)}) copy-start(f32[4,128,128]{2,1,0:T(8,128)S(1)} %get-tuple-element.38) | copy-start | bytes 786436
  32.3 3.8 %copy-start.9 = (f32[4,128,128]{2,1,0:T(8,128)}, f32[4,128,128]{2,1,0:T(8,128)S(1)}, u32[]{:S(2)}) copy-start(f32[4,128,128]{2,1,0:T(8,128)S(1)} %get-tuple-element.41) | copy-start | bytes 786436
  32.3 3.9 %copy-start.7 = (f32[4,128,128]{2,1,0:T(8,128)}, f32[4,128,128]{2,1,0:T(8,128)S(1)}, u32[]{:S(2)}) copy-start(f32[4,128,128]{2,1,0:T(8,128)S(1)} %get-tuple-element.40) | copy-start | bytes 786436
  34.6 7.0 %copy-start.14 = (f32[3,2,64,64]{2,3,1,0:T(8,128)}, f32[3,2,64,64]{2,3,1,0:T(8,128)S(1)}, u32[]{:S(2)}) copy-start(f32[3,2,64,64]{2,3,1,0:T(8,128)S(1)} %fusion.115) | copy-start | bytes 294916
  37.5 5.8 %copy-start.18 = (f32[3,2,64,64]{2,3,1,0:T(8,128)}, f32[3,2,64,64]{2,3,1,0:T(8,128)S(1)}, u32[]{:S(2)}) copy-start(f32[3,2,64,64]{2,3,1,0:T(8,128)S(1)} %fusion.111) | copy-start | bytes 294916
  50.4 2.5 %copy-start.25 = (f32[2,2,64,2,128]{4,2,3,1,0:T(8,128)S(1)}, f32[2,2,64,2,128]{4,2,3,1,0:T(8,128)}, u32[]{:S(2)}) copy-start(f32[2,2,64,2,128]{4,2,3,1,0:T(8,128)} %copy.49) | copy-start | bytes 786436
  50.4 2.5 %copy-start.26 = (f32[2,2,64,2,128]{4,2,3,1,0:T(8,128)S(1)}, f32[2,2,64,2,128]{4,2,3,1,0:T(8,128)}, u32[]{:S(2)}) copy-start(f32[2,2,64,2,128]{4,2,3,1,0:T(8,128)} %copy.50) | copy-start | bytes 786436
  74.8 10.7 %collective-permute-start.12 = (f32[3,1,1,32]{2,3,0,1:T(8,128)S(1)}, f32[3,1,1,32]{2,3,0,1:T(8,128)S(1)}, u32[]{:S(2)}, u32[]{:S(2)}) collective-permute-start(f32[3,1,1,32]{2,3,0,1:T(8,128)S(1)} %get-tuple-element.76), channel_id=1, source_target_pairs={{0,128},{1,129},{2,130},{3,131},{4,132},{5,133},{6,134},{7,135},{8... | collective-permute-start | bytes 1160 | tf_op jit(solution)/shard_map/ppermute | solution.py:20
  76.1 29.1 %collective-permute-start.4 = (f32[3,4,1,128]{3,2,1,0:T(1,128)S(1)}, f32[3,4,1,128]{3,2,1,0:T(1,128)S(1)}, u32[]{:S(2)}, u32[]{:S(2)}) collective-permute-start(f32[3,4,1,128]{3,2,1,0:T(1,128)S(1)} %get-tuple-element.50), channel_id=1, source_target_pairs={{0,128},{1,129},{2,130},{3,131},{4,132},{5,133},{6,134},{7,135},{8... | collective-permute-start | bytes 18440 | tf_op jit(solution)/shard_map/ppermute | solution.py:20
  77.4 13.6 %collective-permute-start.13 = (f32[3,1,1,32]{2,3,0,1:T(8,128)S(1)}, f32[3,1,1,32]{2,3,0,1:T(8,128)S(1)}, u32[]{:S(2)}, u32[]{:S(2)}) collective-permute-start(f32[3,1,1,32]{2,3,0,1:T(8,128)S(1)} %get-tuple-element.77), channel_id=1, source_target_pairs={{128,0},{129,1},{130,2},{131,3},{132,4},{133,5},{134,6},{135,7},{1... | collective-permute-start | bytes 1160 | tf_op jit(solution)/shard_map/ppermute | solution.py:21
  82.9 24.3 %collective-permute-start.5 = (f32[3,4,1,128]{3,2,1,0:T(1,128)S(1)}, f32[3,4,1,128]{3,2,1,0:T(1,128)S(1)}, u32[]{:S(2)}, u32[]{:S(2)}) collective-permute-start(f32[3,4,1,128]{3,2,1,0:T(1,128)S(1)} %get-tuple-element.51), channel_id=1, source_target_pairs={{128,0},{129,1},{130,2},{131,3},{132,4},{133,5},{134,6},{135,7},{1... | collective-permute-start | bytes 18440 | tf_op jit(solution)/shard_map/ppermute | solution.py:21
  84.2 9.8 %collective-permute-start.8 = (f32[3,2,1,64]{2,3,1,0:T(8,128)S(1)}, f32[3,2,1,64]{2,3,1,0:T(8,128)S(1)}, u32[]{:S(2)}, u32[]{:S(2)}) collective-permute-start(f32[3,2,1,64]{2,3,1,0:T(8,128)S(1)} %get-tuple-element.70), channel_id=1, source_target_pairs={{0,128},{1,129},{2,130},{3,131},{4,132},{5,133},{6,134},{7,135},{8... | collective-permute-start | bytes 4616 | tf_op jit(solution)/shard_map/ppermute | solution.py:20
  85.5 10.5 %collective-permute-start.9 = (f32[3,2,1,64]{2,3,1,0:T(8,128)S(1)}, f32[3,2,1,64]{2,3,1,0:T(8,128)S(1)}, u32[]{:S(2)}, u32[]{:S(2)}) collective-permute-start(f32[3,2,1,64]{2,3,1,0:T(8,128)S(1)} %get-tuple-element.71), channel_id=1, source_target_pairs={{128,0},{129,1},{130,2},{131,3},{132,4},{133,5},{134,6},{135,7},{1... | collective-permute-start | bytes 4616 | tf_op jit(solution)/shard_map/ppermute | solution.py:21
  91.1 24.7 %collective-permute-start.14 = (f32[3,1,34,32]{2,3,0,1:T(8,128)S(1)}, f32[3,1,34,32]{2,3,0,1:T(8,128)S(1)}, u32[]{:S(2)}, u32[]{:S(2)}) collective-permute-start(f32[3,1,34,32]{2,3,0,1:T(8,128)S(1)} %pad_maximum_fusion.49), channel_id=1, source_target_pairs={{0,1},{1,2},{2,3},{3,4},{4,5},{5,6},{6,7},{7,8},{8,9},{9,10},{10,1... | collective-permute-start | bytes 39176 | tf_op jit(solution)/shard_map/ppermute | solution.py:20
  94.0 24.0 %collective-permute-start.15 = (f32[3,1,34,32]{2,3,0,1:T(8,128)S(1)}, f32[3,1,34,32]{2,3,0,1:T(8,128)S(1)}, u32[]{:S(2)}, u32[]{:S(2)}) collective-permute-start(f32[3,1,34,32]{2,3,0,1:T(8,128)S(1)} %pad_maximum_fusion.49), channel_id=1, source_target_pairs={{1,0},{2,1},{3,2},{4,3},{5,4},{6,5},{7,6},{8,7},{9,8},{10,9},{11,1... | collective-permute-start | bytes 39176 | tf_op jit(solution)/shard_map/ppermute | solution.py:21
  97.3 21.7 %collective-permute-start.10 = (f32[3,1,66,64]{2,3,1,0:T(8,128)}, f32[3,1,66,64]{2,3,1,0:T(8,128)}, u32[]{:S(2)}, u32[]{:S(2)}) collective-permute-start(f32[3,1,66,64]{2,3,1,0:T(8,128)} %get-tuple-element.68), channel_id=1, source_target_pairs={{0,1},{1,2},{2,3},{3,4},{4,5},{5,6},{6,7},{7,8},{8,9},{9,10},{10,1... | collective-permute-start | bytes 152072 | tf_op jit(solution)/shard_map/ppermute | solution.py:20
  105.2 2.8 %copy-start.37 = (f32[3,4,1,128]{3,2,1,0:T(1,128)}, f32[3,4,1,128]{3,2,1,0:T(1,128)S(1)}, u32[]{:S(2)}) copy-start(f32[3,4,1,128]{3,2,1,0:T(1,128)S(1)} %collective-permute-done.4) | copy-start | bytes 18436
  105.2 13.8 %collective-permute-start.11 = (f32[3,1,66,64]{2,3,1,0:T(8,128)}, f32[3,1,66,64]{2,3,1,0:T(8,128)}, u32[]{:S(2)}, u32[]{:S(2)}) collective-permute-start(f32[3,1,66,64]{2,3,1,0:T(8,128)} %get-tuple-element.69), channel_id=1, source_target_pairs={{1,0},{2,1},{3,2},{4,3},{5,4},{6,5},{7,6},{8,7},{9,8},{10,9},{11,1... | collective-permute-start | bytes 152072 | tf_op jit(solution)/shard_map/ppermute | solution.py:21
  108.0 16.3 %collective-permute-start.6 = (f32[3,1,130,128]{3,2,1,0:T(8,128)}, f32[3,1,130,128]{3,2,1,0:T(8,128)}, u32[]{:S(2)}, u32[]{:S(2)}) collective-permute-start(f32[3,1,130,128]{3,2,1,0:T(8,128)} %get-tuple-element.44), channel_id=1, source_target_pairs={{0,1},{1,2},{2,3},{3,4},{4,5},{5,6},{6,7},{7,8},{8,9},{9,10},{10,1... | collective-permute-start | bytes 599048 | tf_op jit(solution)/shard_map/ppermute | solution.py:20
  115.9 11.7 %collective-permute-start.7 = (f32[3,1,130,128]{3,2,1,0:T(8,128)}, f32[3,1,130,128]{3,2,1,0:T(8,128)}, u32[]{:S(2)}, u32[]{:S(2)}) collective-permute-start(f32[3,1,130,128]{3,2,1,0:T(8,128)} %get-tuple-element.45), channel_id=1, source_target_pairs={{1,0},{2,1},{3,2},{4,3},{5,4},{6,5},{7,6},{8,7},{9,8},{10,9},{11,1... | collective-permute-start | bytes 599048 | tf_op jit(solution)/shard_map/ppermute | solution.py:21
  122.5 6.4 %copy-start.11 = (f32[3,4,128,128]{3,2,1,0:T(8,128)S(1)}, f32[3,4,128,128]{3,2,1,0:T(8,128)}, u32[]{:S(2)}) copy-start(f32[3,4,128,128]{3,2,1,0:T(8,128)} %get-tuple-element.12) | copy-start | bytes 2359300
  (47 other events, 49.5 us)
where the time goes:
time: 135 us; the launch traced here: 134 us
  starting transfers between devices  55.2 us (41%)
  local copies, waits for them, and re-layouts  30.3 us (22%)
  other arithmetic  20.2 us (15%)
  matrix products  15.5 us (11%)
  waiting for transfers between devices  12.2 us (9%)
    ppermute x8, starting transfers between devices, with_halo(): before = lax.ppermute(last, axis, up)  29.5 us
    ppermute x8, starting transfers between devices, with_halo(): after = lax.ppermute(first, axis, down)  25.6 us
    ppermute x8, waiting for transfers between devices, with_halo(): after = lax.ppermute(first, axis, down)  11.8 us
    unnamed x134, local copies, waits for them, and re-layouts  8.04 us
    dot_general x14, matrix products, along_depth(): jnp.einsum('cxyk,kj->cxyj', field, table, precision=lax.Precision.HIGHEST)  7.94 us
    dot_general x2, matrix products, prolong(): jnp.einsum('cxyj,kj->cxyk', spread, table, precision=lax.Precision.HIGHEST)  7.55 us
    div x2, other arithmetic, begin_sweep(): return (relaxation * residual / diagonal, diagonal)  4.7 us
    slice x4, local copies, waits for them, and re-layouts, depth_shift(): return jnp.where(place == 0, 0.0, jnp.roll(array, 1, axis=last))  4.2 us
  transfers between devices with their start and end apart: 16, of which 3 were waited for; matrix products, arithmetic and copies ran while one was open for 9% of the time, Pallas kernels for 0%

commit v1 on v0

v1 whole, which is shorter than its diff:
```python
import functools

import jax
import jax.numpy as jnp
from jax import lax
from jax.experimental import pallas as pl
from jax.experimental.pallas import tpu as pltpu
from jax.sharding import PartitionSpec as P

shear_table = (1.0, 0.6, 1.8, 0.35)
bulk_table = (1.2, 0.9, 2.5, 0.5)
damage_step = 0.25
damage_floor = 0.01
relaxation = 2.0 / 3.0

MESH = pl.DeviceIdType.MESH
X = 4
Y = 128
Z = 128
OFF = 8


def lanes(shape):
    return lax.broadcasted_iota(jnp.int32, shape, len(shape) - 1)


def roll(v, shift):
    return pltpu.roll(v, shift % Z, v.ndim - 1)


def from_above(v, step):
    return jnp.where(lanes(v.shape) < Z - step, roll(v, -step), 0.0)


def from_below(v, step):
    return jnp.where(lanes(v.shape) >= step, roll(v, step), 0.0)


def moduli(phase, damage):
    soft = 1.0 - damage_step * damage.astype(jnp.float32)
    degrade = soft * soft + damage_floor

    def table(values):
        picked = jnp.full(phase.shape, values[3], jnp.float32)
        for label in (2, 1, 0):
            picked = jnp.where(phase == label, values[label], picked)
        return picked

    half = table([0.5 * s for s in shear_table])
    normal = table([0.5 * b + s for s, b in zip(shear_table, bulk_table)])
    return half * degrade, normal * degrade


def kernel(tiles, load_hbm, u_hbm, lab_hbm, dam_hbm, out, U, F, L, INV, R, E, H, K, LAB, DAM, S1, S1R, S2, S2R,
           PS, PR, W2, F2, I2, F3, EX, local_sem, send_sem, recv_sem):
    me = lax.axis_index("tile")
    sec = lax.axis_index("sec")
    has_up = me < tiles - 1
    has_down = me > 0
    up = {"tile": jnp.minimum(me + 1, tiles - 1)}
    down = {"tile": jnp.maximum(me - 1, 0)}
    across = {"sec": 1 - sec}

    loads = [
        pltpu.make_async_copy(lab_hbm, LAB.at[pl.ds(1, X)], local_sem.at[0]),
        pltpu.make_async_copy(dam_hbm, DAM.at[pl.ds(1, X)], local_sem.at[1]),
        pltpu.make_async_copy(u_hbm, U.at[:, pl.ds(1, X), pl.ds(OFF, Y)], local_sem.at[2]),
        pltpu.make_async_copy(load_hbm, L, local_sem.at[3]),
    ]
    for copy in loads:
        copy.start()

    barrier = pltpu.get_barrier_semaphore()

    @pl.when(has_up)
    def _():
        pl.semaphore_signal(barrier, inc=1, device_id=up, device_id_type=MESH)

    @pl.when(has_down)
    def _():
        pl.semaphore_signal(barrier, inc=1, device_id=down, device_id_type=MESH)

    pl.semaphore_signal(barrier, inc=1, device_id=across, device_id_type=MESH)
    pl.semaphore_wait(barrier, 1 + has_up.astype(jnp.int32) + has_down.astype(jnp.int32))

    def remote(src, dst, index, device):
        return pltpu.make_async_remote_copy(
            src_ref=src, dst_ref=dst, send_sem=send_sem.at[index], recv_sem=recv_sem.at[index],
            device_id=device, device_id_type=MESH)

    rows = pl.ds(OFF, Y)
    ups = [
        remote(lab_hbm.at[X - 1], LAB.at[0], 0, up),
        remote(dam_hbm.at[X - 1], DAM.at[0], 1, up),
        remote(u_hbm.at[:, X - 1], U.at[:, 0, rows], 2, up),
    ]
    downs = [
        remote(lab_hbm.at[0], LAB.at[X + 1], 3, down),
        remote(dam_hbm.at[0], DAM.at[X + 1], 4, down),
        remote(u_hbm.at[:, 0], U.at[:, X + 1, rows], 5, down),
    ]

    @pl.when(has_up)
    def _():
        for copy in ups:
            copy.start()

    @pl.when(has_down)
    def _():
        for copy in downs:
            copy.start()

    loads[0].wait()
    loads[1].wait()

    @pl.loop(0, Y // 8)
    def _(i):
        y = pl.multiple_of(i * 8, 8)
        for p in range(1, X + 1):
            h, k = moduli(LAB[p, pl.ds(y, 8), :], DAM[p, pl.ds(y, 8), :])
            H[p, pl.ds(OFF + y, 8), :] = h
            K[p, pl.ds(OFF + y, 8), :] = k

    loads[2].wait()

    own_row = jnp.where(sec == 0, OFF + Y - 1, OFF)
    halo_row = jnp.where(sec == 0, OFF + Y, OFF - 1)
    edge_row = jnp.where(sec == 0, OFF - 1, OFF + Y)
    faces = [H.at[pl.ds(1, X)], K.at[pl.ds(1, X)]] + [U.at[c, pl.ds(1, X)] for c in range(3)]
    for f, ref in enumerate(faces):
        for p in range(X):
            S1[pl.ds(X * f + p, 1), :] = ref[p, pl.ds(own_row, 1), :]
    for r in range(20, 24):
        S1[pl.ds(r, 1), :] = jnp.zeros((1, Z), jnp.float32)
    cross1 = remote(S1, S1R, 6, across)
    cross1.start()
    zero_row = jnp.zeros((1, Z), jnp.float32)
    for ref in faces:
        for p in range(X):
            ref[p, pl.ds(edge_row, 1), :] = zero_row
    for c in range(3):
        for p in range(1, X + 1):
            F[c, p, pl.ds(edge_row, 1), :] = zero_row

    @pl.when(jnp.logical_not(has_down))
    def _():
        H[0] = jnp.zeros(H.shape[1:], jnp.float32)
        K[0] = jnp.zeros(K.shape[1:], jnp.float32)
        for c in range(3):
            U[c, 0] = jnp.zeros(U.shape[2:], jnp.float32)
            F[c, 0] = jnp.zeros(F.shape[2:], jnp.float32)

    @pl.when(jnp.logical_not(has_up))
    def _():
        H[X + 1] = jnp.zeros(H.shape[1:], jnp.float32)
        K[X + 1] = jnp.zeros(K.shape[1:], jnp.float32)
        for c in range(3):
            U[c, X + 1] = jnp.zeros(U.shape[2:], jnp.float32)
            F[c, X + 1] = jnp.zeros(F.shape[2:], jnp.float32)

    loads[3].wait()
    cross1.wait()
    for f, ref in enumerate(faces):
        for p in range(X):
            ref[p, pl.ds(halo_row, 1), :] = S1R[pl.ds(X * f + p, 1), :]

    def weights(p, y):
        result = {}
        for name, M in (("s", H), ("t", K)):
            m = M[p, pl.ds(OFF + y, 8), :]
            if p > 1:
                result[name, "xl"] = m + M[p - 1, pl.ds(OFF + y, 8), :]
            if p < X:
                result[name, "xu"] = m + M[p + 1, pl.ds(OFF + y, 8), :]
            result[name, "yl"] = m + M[p, pl.ds(OFF + y - 1, 8), :]
            result[name, "yu"] = m + M[p, pl.ds(OFF + y + 1, 8), :]
            result[name, "zl"] = m + from_below(m, 1)
            result[name, "zu"] = m + from_above(m, 1)
        return result

    def neighbours(V, c, p, y, w):
        v = V[c, p, pl.ds(OFF + y, 8), :]
        kind = ["t" if c == a else "s" for a in range(3)]
        total = w[kind[1], "yl"] * V[c, p, pl.ds(OFF + y - 1, 8), :]
        total = total + w[kind[1], "yu"] * V[c, p, pl.ds(OFF + y + 1, 8), :]
        total = total + w[kind[2], "zl"] * from_below(v, 1)
        total = total + w[kind[2], "zu"] * from_above(v, 1)
        if p > 1:
            total = total + w[kind[0], "xl"] * V[c, p - 1, pl.ds(OFF + y, 8), :]
        if p < X:
            total = total + w[kind[0], "xu"] * V[c, p + 1, pl.ds(OFF + y, 8), :]
        return total, v

    @pl.loop(0, Y // 8)
    def _(i):
        y = pl.multiple_of(i * 8, 8)
        here = pl.ds(y, 8)
        for p in range(1, X + 1):
            w = weights(p, y)
            sides = {}
            for name in ("s", "t"):
                xs = [w[name, side] for side in ("xl", "xu") if (name, side) in w]
                sides[name, 0] = xs[0] if len(xs) == 1 else xs[0] + xs[1]
                sides[name, 1] = w[name, "yl"] + w[name, "yu"]
                sides[name, 2] = w[name, "zl"] + w[name, "zu"]
            for c in range(3):
                total, v = neighbours(U, c, p, y, w)
                others = [a for a in range(3) if a != c]
                diag = sides["t", c] + sides["s", others[0]] + sides["s", others[1]]
                acc = L[c, p - 1, here, :] + total
                if 1 < p < X:
                    r = acc - diag * v
                    inv = relaxation / diag
                    R[c, p - 2, here, :] = r
                    INV[c, p - 1, here, :] = inv
                    F[c, p, pl.ds(OFF + y, 8), :] = r * inv
                else:
                    L[c, p - 1, here, :] = acc
                    INV[c, p - 1, here, :] = diag

    @pl.when(has_down)
    def _():
        for copy in ups:
            copy.wait_recv()

    @pl.when(has_up)
    def _():
        for copy in downs:
            copy.wait_recv()

    @pl.loop(0, Y // 8)
    def _(i):
        y = pl.multiple_of(i * 8, 8)
        here = pl.ds(y, 8)
        there = pl.ds(OFF + y, 8)
        for p, q, present in ((1, 0, has_down), (X, X + 1, has_up)):
            h, k = moduli(LAB[q, here, :], DAM[q, here, :])
            scale = present.astype(jnp.float32)
            h = jnp.where(present, h, 0.0)
            k = jnp.where(present, k, 0.0)
            H[q, there, :] = h
            K[q, there, :] = k
            s = h + H[p, there, :]
            t = k + K[p, there, :]
            for c in range(3):
                w = t if c == 0 else s
                diag = INV[c, p - 1, here, :] + w
                r = L[c, p - 1, here, :] + w * U[c, q, there, :] - diag * U[c, p, there, :]
                inv = relaxation / diag
                INV[c, p - 1, here, :] = inv
                F[c, p, there, :] = r * inv
                R[c, (p - 1) // 2, here, :] = R[c, (p - 1) // 2, here, :] + r

    f_up = remote(F.at[:, X, rows], F.at[:, 0, rows], 7, up)
    f_down = remote(F.at[:, 1, rows], F.at[:, X + 1, rows], 8, down)

    @pl.when(has_up)
    def _():
        f_up.start()

    @pl.when(has_down)
    def _():
        f_down.start()

    Y2, Y3 = Y // 2, Y // 4
    shape2, shape3 = (Y2, Z), (Y3, Z)
    odd2 = (lanes(shape2) & 1) == 1

    def pairs(v):
        return v + jnp.where(odd2, roll(v, 1), roll(v, -1))

    def every_other(M, p, first):
        return M[p, pl.ds(first, Y2, stride=2), :]

    for m, M in enumerate((H, K)):
        for j in range(3):
            face = every_other(M, 2 * j, OFF) + every_other(M, 2 * j, OFF + 1)
            face = face + every_other(M, 2 * j + 1, OFF) + every_other(M, 2 * j + 1, OFF + 1)
            W2[m, j] = pairs(face)
        for j in range(2):
            r7, r8, r9, r10 = [
                every_other(M, 1 + 2 * j, OFF + d) + every_other(M, 2 + 2 * j, OFF + d) for d in (-1, 0, 1, 2)]
            W2[m, 3 + j] = pairs(r7 + r8)
            W2[m, 5 + j] = pairs(r9 + r10)
            cell = r8 + r9
            low = cell + from_below(cell, 1)
            high = cell + from_above(cell, 1)
            W2[m, 7 + j] = jnp.where(odd2, roll(low, 1), low)
            W2[m, 9 + j] = jnp.where(odd2, high, roll(high, -1))

    def kinds(c):
        return [1 if c == a else 0 for a in range(3)]

    for c in range(3):
        kx, ky, kz = kinds(c)
        for j in range(2):
            diag = W2[kx, j] + W2[kx, j + 1] + W2[ky, 3 + j] + W2[ky, 5 + j] + W2[kz, 7 + j] + W2[kz, 9 + j]
            inv = relaxation / diag
            I2[c, j] = inv
            res = R[c, j, pl.ds(0, Y2, stride=2), :] + R[c, j, pl.ds(1, Y2, stride=2), :]
            res = pairs(res)
            EX[c, j] = res
            F2[c, 1 + j, pl.ds(OFF, Y2), :] = res * inv

    quad = lanes(shape3) & 3
    high3 = quad >= 2

    def quads(v):
        return v + jnp.where(high3, roll(v, 2), roll(v, -2))

    def row_of(m, slot, first):
        return W2[m, slot, pl.ds(first, Y3, stride=2), :]

    w3 = {}
    for m in range(2):
        w3[m, "xl"] = quads(row_of(m, 0, 0) + row_of(m, 0, 1))
        w3[m, "xu"] = quads(row_of(m, 2, 0) + row_of(m, 2, 1))
        w3[m, "yl"] = quads(row_of(m, 3, 0) + row_of(m, 4, 0))
        w3[m, "yu"] = quads(row_of(m, 5, 1) + row_of(m, 6, 1))
        low = row_of(m, 7, 0) + row_of(m, 7, 1) + row_of(m, 8, 0) + row_of(m, 8, 1)
        high = row_of(m, 9, 0) + row_of(m, 9, 1) + row_of(m, 10, 0) + row_of(m, 10, 1)
        w3[m, "zl"] = jnp.where(high3, roll(low, 2), low)
        w3[m, "zu"] = jnp.where(high3, high, roll(high, -2))
    inv3 = []
    for c in range(3):
        kx, ky, kz = kinds(c)
        diag = w3[kx, "xl"] + w3[kx, "xu"] + w3[ky, "yl"] + w3[ky, "yu"] + w3[kz, "zl"] + w3[kz, "zu"]
        inv3.append(relaxation / diag)
        res = EX[c, 0, pl.ds(0, Y3, stride=2), :] + EX[c, 0, pl.ds(1, Y3, stride=2), :]
        res = res + EX[c, 1, pl.ds(0, Y3, stride=2), :] + EX[c, 1, pl.ds(1, Y3, stride=2), :]
        F3[c, 1, pl.ds(OFF, Y3), :] = quads(res) * inv3[c]

    half = Y2 // 2
    odd_half = odd2[:half]
    quad8 = quad[:8]
    for side, p2 in ((0, 2), (1, 1)):
        for c in range(3):
            a = F2[c, p2, pl.ds(OFF, half), :]
            b = F2[c, p2, pl.ds(OFF + half, half), :]
            PS[side, pl.ds(half * c, half), :] = jnp.where(odd_half, b, a)
            v = F3[c, 1, pl.ds(OFF, 8), :]
            for q in range(1, 4):
                v = jnp.where(quad8 == q, F3[c, 1, pl.ds(OFF + 8 * q, 8), :], v)
            PS[side, pl.ds(3 * half + 8 * c, 8), :] = v
    c_up = remote(PS.at[0], PR.at[0], 9, up)
    c_down = remote(PS.at[1], PR.at[1], 10, down)

    @pl.when(has_up)
    def _():
        c_up.start()

    @pl.when(has_down)
    def _():
        c_down.start()

    own2 = jnp.where(sec == 0, OFF + Y2 - 1, OFF)
    own3 = jnp.where(sec == 0, OFF + Y3 - 1, OFF)
    halo2 = jnp.where(sec == 0, OFF + Y2, OFF - 1)
    halo3 = jnp.where(sec == 0, OFF + Y3, OFF - 1)
    edge2 = jnp.where(sec == 0, OFF - 1, OFF + Y2)
    edge3 = jnp.where(sec == 0, OFF - 1, OFF + Y3)
    face_rows = []
    for c in range(3):
        for p in range(1, X + 1):
            face_rows.append((F, c, p, own_row, halo_row))
        for p in (1, 2):
            face_rows.append((F2, c, p, own2, halo2))
            F2[c, p, pl.ds(edge2, 1), :] = zero_row
        face_rows.append((F3, c, 1, own3, halo3))
        F3[c, 1, pl.ds(edge3, 1), :] = zero_row
    for r, (V, c, p, own, halo) in enumerate(face_rows):
        S2[pl.ds(r, 1), :] = V[c, p, pl.ds(own, 1), :]
    for r in range(21, 24):
        S2[pl.ds(r, 1), :] = zero_row
    cross2 = remote(S2, S2R, 11, across)
    cross2.start()
    cross2.wait()
    for r, (V, c, p, own, halo) in enumerate(face_rows):
        V[c, p, pl.ds(halo, 1), :] = S2R[pl.ds(r, 1), :]

    @pl.loop(0, Y // 8)
    def _(i):
        y = pl.multiple_of(i * 8, 8)
        here = pl.ds(y, 8)
        for p in range(1, X + 1):
            w = weights(p, y)
            for c in range(3):
                total, v = neighbours(F, c, p, y, w)
                E[c, p - 1, here, :] = (4.0 / 3.0) * v + INV[c, p - 1, here, :] * total

    @pl.when(has_down)
    def _():
        f_up.wait_recv()
        c_up.wait_recv()

    @pl.when(has_up)
    def _():
        f_down.wait_recv()
        c_down.wait_recv()

    for side, p2, p3, present in ((0, 0, 0, has_down), (1, 3, 2, has_up)):
        for c in range(3):
            v = jnp.where(present, PR[side, pl.ds(half * c, half), :], 0.0)
            F2[c, p2, pl.ds(OFF, half), :] = jnp.where(odd_half, roll(v, 1), v)
            F2[c, p2, pl.ds(OFF + half, half), :] = jnp.where(odd_half, v, roll(v, -1))
            v = jnp.where(present, PR[side, pl.ds(3 * half + 8 * c, 8), :], 0.0)
            for q in range(4):
                spread = v
                for lane in range(4):
                    if lane != q:
                        spread = jnp.where(quad8 == lane, roll(v, lane - q), spread)
                F3[c, p3, pl.ds(OFF + 8 * q, 8), :] = spread

    for c in range(3):
        kx, ky, kz = kinds(c)
        v = F3[c, 1, pl.ds(OFF, Y3), :]
        total = w3[kx, "xl"] * F3[c, 0, pl.ds(OFF, Y3), :] + w3[kx, "xu"] * F3[c, 2, pl.ds(OFF, Y3), :]
        total = total + w3[ky, "yl"] * F3[c, 1, pl.ds(OFF - 1, Y3), :] + w3[ky, "yu"] * F3[c, 1, pl.ds(OFF + 1, Y3), :]
        total = total + w3[kz, "zl"] * from_below(v, 4) + w3[kz, "zu"] * from_above(v, 4)
        e3 = (4.0 / 3.0) * v + inv3[c] * total
        EX[c, 0, pl.ds(0, Y3, stride=2), :] = e3
        EX[c, 0, pl.ds(1, Y3, stride=2), :] = e3
        e3 = EX[c, 0]
        for j in range(2):
            p = 1 + j
            v = F2[c, p, pl.ds(OFF, Y2), :]
            total = W2[kx, j] * F2[c, p - 1, pl.ds(OFF, Y2), :] + W2[kx, j + 1] * F2[c, p + 1, pl.ds(OFF, Y2), :]
            total = total + W2[ky, 3 + j] * F2[c, p, pl.ds(OFF - 1, Y2), :]
            total = total + W2[ky, 5 + j] * F2[c, p, pl.ds(OFF + 1, Y2), :]
            total = total + W2[kz, 7 + j] * from_below(v, 2) + W2[kz, 9 + j] * from_above(v, 2)
            e2 = (4.0 / 3.0) * v + I2[c, j] * total + e3
            R[c, j, pl.ds(0, Y2, stride=2), :] = e2
            R[c, j, pl.ds(1, Y2, stride=2), :] = e2

    @pl.loop(0, Y // 8)
    def _(i):
        y = pl.multiple_of(i * 8, 8)
        here = pl.ds(y, 8)
        there = pl.ds(OFF + y, 8)
        for p, q in ((1, 0), (2, None), (3, None), (4, X + 1)):
            if q is not None:
                s = H[q, there, :] + H[p, there, :]
                t = K[q, there, :] + K[p, there, :]
            for c in range(3):
                value = E[c, p - 1, here, :] + R[c, (p - 1) // 2, here, :]
                if q is not None:
                    w = t if c == 0 else s
                    value = value + INV[c, p - 1, here, :] * (w * F[c, q, there, :])
                out[c, p - 1, here, :] = value

    @pl.when(has_up)
    def _():
        for copy in ups + [f_up, c_up]:
            copy.wait_send()

    @pl.when(has_down)
    def _():
        for copy in downs + [f_down, c_down]:
            copy.wait_send()


def per_device(tiles, load_field, iterate, phase_label, damage):
    f32, i32 = jnp.float32, jnp.int32
    padded = Y + 2 * OFF
    return pl.pallas_call(
        functools.partial(kernel, tiles),
        out_shape=jax.ShapeDtypeStruct(load_field.shape, f32),
        in_specs=[pl.BlockSpec(memory_space=pl.ANY)] * 4,
        out_specs=pl.BlockSpec(memory_space=pltpu.VMEM),
        scratch_shapes=[
            pltpu.VMEM((3, X + 2, padded, Z), f32),
            pltpu.VMEM((3, X + 2, padded, Z), f32),
            pltpu.VMEM((3, X, Y, Z), f32),
            pltpu.VMEM((3, X, Y, Z), f32),
            pltpu.VMEM((3, X // 2, Y, Z), f32),
            pltpu.VMEM((3, X, Y, Z), f32),
            pltpu.VMEM((X + 2, padded, Z), f32),
            pltpu.VMEM((X + 2, padded, Z), f32),
            pltpu.VMEM((X + 2, Y, Z), i32),
            pltpu.VMEM((X + 2, Y, Z), i32),
            pltpu.VMEM((24, Z), f32),
            pltpu.VMEM((24, Z), f32),
            pltpu.VMEM((24, Z), f32),
            pltpu.VMEM((24, Z), f32),
            pltpu.VMEM((2, 120, Z), f32),
            pltpu.VMEM((2, 120, Z), f32),
            pltpu.VMEM((2, 11, Y // 2, Z), f32),
            pltpu.VMEM((3, 4, Y // 2 + 2 * OFF, Z), f32),
            pltpu.VMEM((3, 2, Y // 2, Z), f32),
            pltpu.VMEM((3, 3, Y // 4 + 2 * OFF, Z), f32),
            pltpu.VMEM((3, 2, Y // 2, Z), f32),
            pltpu.SemaphoreType.DMA((4,)),
            pltpu.SemaphoreType.DMA((12,)),
            pltpu.SemaphoreType.DMA((12,)),
        ],
        compiler_params=pltpu.CompilerParams(
            collective_id=0, has_side_effects=True, vmem_limit_bytes=48 * 1024 * 1024),
    )(load_field, iterate, phase_label, damage)


def solution(mesh):
    tiles = mesh.shape["tile"]
    in_specs = (
        P(None, "tile", "sec", None),
        P(None, "tile", "sec", None),
        P("tile", "sec", None),
        P("tile", "sec", None),
    )
    out_specs = P(None, "tile", "sec", None)
    return jax.shard_map(
        functools.partial(per_device, tiles), mesh=mesh, in_specs=in_specs, out_specs=out_specs, check_vma=False
    )
```

time: 135 us -> 30.5 us (0.23)
  the two profiles are of different devices: /device:TPU:127 before, /device:TPU:1 now
where the time goes in v1:
time: 30.5 us; the launch traced here: 30.3 us
  Pallas kernels  25.2 us (83%)
  local copies, waits for them, and re-layouts  5.05 us (17%)
    pallas_call x1, Pallas kernels, per_device(): pl.pallas_call(functools.partial(kernel, tiles), out_shape=jax.ShapeDtype...  25.2 us
    unnamed x9, local copies, waits for them, and re-layouts  5.05 us

profile of v1, /device:TPU:1, one launch (start us, length us, event | category | flops | bytes accessed | tf_op | source)
XLA Modules:
  0.0 30.3 jit_solution(566984319464254448)
XLA Ops:
  0.0 0.0 copy-start
  0.0 1.1 %copy-done = f32[3,4,128,128]{3,2,1,0:T(8,128)S(1)} copy-done((f32[3,4,128,128]{3,2,1,0:T(8,128)S(1)}, f32[3,4,128,128]{3,2,1,0:T(8,128)}, u32[]{:S(2)}) %copy-start) | copy-done | bytes 786456
  1.1 0.0 copy-start.1
  1.1 1.1 %copy-done.1 = f32[3,4,128,128]{3,2,1,0:T(8,128)S(1)} copy-done((f32[3,4,128,128]{3,2,1,0:T(8,128)S(1)}, f32[3,4,128,128]{3,2,1,0:T(8,128)}, u32[]{:S(2)}) %copy-start.1) | copy-done | bytes 786456
  2.3 0.0 copy-start.2
  2.3 0.9 %copy-done.2 = s32[4,128,128]{2,1,0:T(8,128)S(1)} copy-done((s32[4,128,128]{2,1,0:T(8,128)S(1)}, s32[4,128,128]{2,1,0:T(8,128)}, u32[]{:S(2)}) %copy-start.2) | copy-done | bytes 262168
  3.2 0.0 copy-start.3
  3.2 0.9 %copy-done.3 = s32[4,128,128]{2,1,0:T(8,128)S(1)} copy-done((s32[4,128,128]{2,1,0:T(8,128)S(1)}, s32[4,128,128]{2,1,0:T(8,128)}, u32[]{:S(2)}) %copy-start.3) | copy-done | bytes 262168
  4.2 25.2 %shard_map.46 = f32[3,4,128,128]{3,2,1,0:T(8,128)S(1)} custom-call(f32[3,4,128,128]{3,2,1,0:T(8,128)S(1)} %copy-done, f32[3,4,128,128]{3,2,1,0:T(8,128)S(1)} %copy-done.1, s32[4,128,128]{2,1,0:T(8,128)S(1)} %copy-done.2, s32[4,128,128]{2,1,0:T(8,128)S(1)} %copy-done.3), custom_call_target="tpu_custom_call" | custom-call | tf_op jit(solution)/shard_map/pallas_call | solution.py:465
  29.4 0.9 %copy.6 = f32[3,4,128,128]{3,2,1,0:T(8,128)} copy(f32[3,4,128,128]{3,2,1,0:T(8,128)S(1)} %shard_map.46) | data formatting | bytes 1572864
Async XLA Ops:
  0.0 1.1 %copy-start = (f32[3,4,128,128]{3,2,1,0:T(8,128)S(1)}, f32[3,4,128,128]{3,2,1,0:T(8,128)}, u32[]{:S(2)}) copy-start(f32[3,4,128,128]{3,2,1,0:T(8,128)} %load_hbm.1) | copy-start | bytes 2359300
  1.1 1.1 %copy-start.1 = (f32[3,4,128,128]{3,2,1,0:T(8,128)S(1)}, f32[3,4,128,128]{3,2,1,0:T(8,128)}, u32[]{:S(2)}) copy-start(f32[3,4,128,128]{3,2,1,0:T(8,128)} %u_hbm.1) | copy-start | bytes 2359300
  2.3 0.9 %copy-start.2 = (s32[4,128,128]{2,1,0:T(8,128)S(1)}, s32[4,128,128]{2,1,0:T(8,128)}, u32[]{:S(2)}) copy-start(s32[4,128,128]{2,1,0:T(8,128)} %lab_hbm.1) | copy-start | bytes 786436
  3.2 0.9 %copy-start.3 = (s32[4,128,128]{2,1,0:T(8,128)S(1)}, s32[4,128,128]{2,1,0:T(8,128)}, u32[]{:S(2)}) copy-start(s32[4,128,128]{2,1,0:T(8,128)} %dam_hbm.1) | copy-start | bytes 786436

commit v2 on v1

--- a/solution.py
+++ b/solution.py
@@ -17,6 +17,7 @@
 X = 4
 Y = 128
 Z = 128
+PARTS = 4
 OFF = 8
 
 
@@ -55,11 +56,22 @@
            PS, PR, W2, F2, I2, F3, EX, local_sem, send_sem, recv_sem):
     me = lax.axis_index("tile")
     sec = lax.axis_index("sec")
-    has_up = me < tiles - 1
-    has_down = me > 0
-    up = {"tile": jnp.minimum(me + 1, tiles - 1)}
-    down = {"tile": jnp.maximum(me - 1, 0)}
+    odd = lax.rem(me, 2)
+    has_far = jnp.logical_and(me > 0, me < tiles - 1)
+    near = {"tile": me + 1 - 2 * odd}
+    far = {"tile": jnp.clip(me - 1 + 2 * odd, 0, tiles - 1)}
     across = {"sec": 1 - sec}
+    p_near, q_near = X - (X - 1) * odd, (X + 1) * (1 - odd)
+    p_far, q_far = 1 + (X - 1) * odd, (X + 1) * odd
+
+    barrier = pltpu.get_barrier_semaphore()
+    pl.semaphore_signal(barrier, inc=1, device_id=near, device_id_type=MESH)
+
+    @pl.when(has_far)
+    def _():
+        pl.semaphore_signal(barrier, inc=1, device_id=far, device_id_type=MESH)
+
+    pl.semaphore_signal(barrier, inc=1, device_id=across, device_id_type=MESH)
 
     loads = [
         pltpu.make_async_copy(lab_hbm, LAB.at[pl.ds(1, X)], local_sem.at[0]),
@@ -70,18 +82,24 @@
     for copy in loads:
         copy.start()
 
-    barrier = pltpu.get_barrier_semaphore()
-
-    @pl.when(has_up)
-    def _():
-        pl.semaphore_signal(barrier, inc=1, device_id=up, device_id_type=MESH)
-
-    @pl.when(has_down)
-    def _():
-        pl.semaphore_signal(barrier, inc=1, device_id=down, device_id_type=MESH)
-
-    pl.semaphore_signal(barrier, inc=1, device_id=across, device_id_type=MESH)
-    pl.semaphore_wait(barrier, 1 + has_up.astype(jnp.int32) + has_down.astype(jnp.int32))
+    own_row = jnp.where(sec == 0, OFF + Y - 1, OFF)
+    halo_row = jnp.where(sec == 0, OFF + Y, OFF - 1)
+    edge_row = jnp.where(sec == 0, OFF - 1, OFF + Y)
+    faces = [H.at[pl.ds(1, X)], K.at[pl.ds(1, X)]] + [U.at[c, pl.ds(1, X)] for c in range(3)]
+    zero_row = jnp.zeros((1, Z), jnp.float32)
+    for r in range(20, 24):
+        S1[pl.ds(r, 1), :] = zero_row
+    for copy in loads[:2]:
+        copy.wait()
+    for p in range(X):
+        h, k = moduli(LAB[1 + p, pl.ds(own_row - OFF, 1), :], DAM[1 + p, pl.ds(own_row - OFF, 1), :])
+        S1[pl.ds(p, 1), :] = h
+        S1[pl.ds(X + p, 1), :] = k
+    loads[2].wait()
+    for f in range(2, 5):
+        for p in range(X):
+            S1[pl.ds(X * f + p, 1), :] = faces[f][p, pl.ds(own_row, 1), :]
+    pl.semaphore_wait(barrier, 2 + has_far.astype(jnp.int32))
 
     def remote(src, dst, index, device):
         return pltpu.make_async_remote_copy(
@@ -89,29 +107,33 @@
             device_id=device, device_id_type=MESH)
 
     rows = pl.ds(OFF, Y)
-    ups = [
-        remote(lab_hbm.at[X - 1], LAB.at[0], 0, up),
-        remote(dam_hbm.at[X - 1], DAM.at[0], 1, up),
-        remote(u_hbm.at[:, X - 1], U.at[:, 0, rows], 2, up),
+    part = Y // PARTS
+    far1 = []
+    for n in range(PARTS):
+        here, there = pl.ds(n * part, part), pl.ds(OFF + n * part, part)
+        far1.append([
+            remote(lab_hbm.at[p_far - 1, here], LAB.at[X + 1 - q_far, here], 3 * n, far),
+            remote(dam_hbm.at[p_far - 1, here], DAM.at[X + 1 - q_far, here], 3 * n + 1, far),
+            remote(u_hbm.at[:, p_far - 1, here], U.at[:, X + 1 - q_far, there], 3 * n + 2, far),
+        ])
+    base = 3 * PARTS
+    near1 = [
+        remote(lab_hbm.at[p_near - 1], LAB.at[X + 1 - q_near], base, near),
+        remote(dam_hbm.at[p_near - 1], DAM.at[X + 1 - q_near], base + 1, near),
+        remote(u_hbm.at[:, p_near - 1], U.at[:, X + 1 - q_near, rows], base + 2, near),
     ]
-    downs = [
-        remote(lab_hbm.at[0], LAB.at[X + 1], 3, down),
-        remote(dam_hbm.at[0], DAM.at[X + 1], 4, down),
-        remote(u_hbm.at[:, 0], U.at[:, X + 1, rows], 5, down),
-    ]
-
-    @pl.when(has_up)
+
+    cross1 = remote(S1, S1R, base + 3, across)
+    cross1.start()
+
+    @pl.when(has_far)
     def _():
-        for copy in ups:
-            copy.start()
-
-    @pl.when(has_down)
-    def _():
-        for copy in downs:
-            copy.start()
-
-    loads[0].wait()
-    loads[1].wait()
+        for copies in far1:
+            for copy in copies:
+                copy.start()
+
+    for copy in near1:
+        copy.start()
 
     @pl.loop(0, Y // 8)
     def _(i):
@@ -121,20 +143,6 @@
             H[p, pl.ds(OFF + y, 8), :] = h
             K[p, pl.ds(OFF + y, 8), :] = k
 
-    loads[2].wait()
-
-    own_row = jnp.where(sec == 0, OFF + Y - 1, OFF)
-    halo_row = jnp.where(sec == 0, OFF + Y, OFF - 1)
-    edge_row = jnp.where(sec == 0, OFF - 1, OFF + Y)
-    faces = [H.at[pl.ds(1, X)], K.at[pl.ds(1, X)]] + [U.at[c, pl.ds(1, X)] for c in range(3)]
-    for f, ref in enumerate(faces):
-        for p in range(X):
-            S1[pl.ds(X * f + p, 1), :] = ref[p, pl.ds(own_row, 1), :]
-    for r in range(20, 24):
-        S1[pl.ds(r, 1), :] = jnp.zeros((1, Z), jnp.float32)
-    cross1 = remote(S1, S1R, 6, across)
-    cross1.start()
-    zero_row = jnp.zeros((1, Z), jnp.float32)
     for ref in faces:
         for p in range(X):
             ref[p, pl.ds(edge_row, 1), :] = zero_row
@@ -142,27 +150,13 @@
         for p in range(1, X + 1):
             F[c, p, pl.ds(edge_row, 1), :] = zero_row
 
-    @pl.when(jnp.logical_not(has_down))
+    @pl.when(jnp.logical_not(has_far))
     def _():
-        H[0] = jnp.zeros(H.shape[1:], jnp.float32)
-        K[0] = jnp.zeros(K.shape[1:], jnp.float32)
+        for ref in (H, K):
+            ref[q_far] = jnp.zeros(H.shape[1:], jnp.float32)
         for c in range(3):
-            U[c, 0] = jnp.zeros(U.shape[2:], jnp.float32)
-            F[c, 0] = jnp.zeros(F.shape[2:], jnp.float32)
-
-    @pl.when(jnp.logical_not(has_up))
-    def _():
-        H[X + 1] = jnp.zeros(H.shape[1:], jnp.float32)
-        K[X + 1] = jnp.zeros(K.shape[1:], jnp.float32)
-        for c in range(3):
-            U[c, X + 1] = jnp.zeros(U.shape[2:], jnp.float32)
-            F[c, X + 1] = jnp.zeros(F.shape[2:], jnp.float32)
-
-    loads[3].wait()
-    cross1.wait()
-    for f, ref in enumerate(faces):
-        for p in range(X):
-            ref[p, pl.ds(halo_row, 1), :] = S1R[pl.ds(X * f + p, 1), :]
+            U[c, q_far] = jnp.zeros(U.shape[2:], jnp.float32)
+            F[c, q_far] = jnp.zeros(F.shape[2:], jnp.float32)
 
     def weights(p, y):
         result = {}
@@ -191,9 +185,7 @@
             total = total + w[kind[0], "xu"] * V[c, p + 1, pl.ds(OFF + y, 8), :]
         return total, v
 
-    @pl.loop(0, Y // 8)
-    def _(i):
-        y = pl.multiple_of(i * 8, 8)
+    def inner_residual(y):
         here = pl.ds(y, 8)
         for p in range(1, X + 1):
             w = weights(p, y)
@@ -218,49 +210,67 @@
                     L[c, p - 1, here, :] = acc
                     INV[c, p - 1, here, :] = diag
 
-    @pl.when(has_down)
-    def _():
-        for copy in ups:
-            copy.wait_recv()
-
-    @pl.when(has_up)
-    def _():
-        for copy in downs:
-            copy.wait_recv()
+    halo_chunk = pl.multiple_of((1 - sec) * (Y - 8), 8)
+    loads[3].wait()
+
+    @pl.loop(0, Y // 8 - 1)
+    def _(i):
+        inner_residual(pl.multiple_of((i + sec) * 8, 8))
+
+    cross1.wait()
+    for f, ref in enumerate(faces):
+        for p in range(X):
+            ref[p, pl.ds(halo_row, 1), :] = S1R[pl.ds(X * f + p, 1), :]
+    inner_residual(halo_chunk)
+
+    def outer_face(p, q, y, present):
+        here, there = pl.ds(y, 8), pl.ds(OFF + y, 8)
+        h, k = moduli(LAB[q, here, :], DAM[q, here, :])
+        if present is not None:
+            h = jnp.where(present, h, 0.0)
+            k = jnp.where(present, k, 0.0)
+        H[q, there, :] = h
+        K[q, there, :] = k
+        s = h + H[p, there, :]
+        t = k + K[p, there, :]
+        j = (p - 1) // 2
+        for c in range(3):
+            w = t if c == 0 else s
+            diag = INV[c, p - 1, here, :] + w
+            r = L[c, p - 1, here, :] + w * U[c, q, there, :] - diag * U[c, p, there, :]
+            inv = relaxation / diag
+            INV[c, p - 1, here, :] = inv
+            F[c, p, there, :] = r * inv
+            R[c, j, here, :] = R[c, j, here, :] + r
+
+    for copy in near1:
+        copy.wait_recv()
 
     @pl.loop(0, Y // 8)
     def _(i):
-        y = pl.multiple_of(i * 8, 8)
-        here = pl.ds(y, 8)
-        there = pl.ds(OFF + y, 8)
-        for p, q, present in ((1, 0, has_down), (X, X + 1, has_up)):
-            h, k = moduli(LAB[q, here, :], DAM[q, here, :])
-            scale = present.astype(jnp.float32)
-            h = jnp.where(present, h, 0.0)
-            k = jnp.where(present, k, 0.0)
-            H[q, there, :] = h
-            K[q, there, :] = k
-            s = h + H[p, there, :]
-            t = k + K[p, there, :]
-            for c in range(3):
-                w = t if c == 0 else s
-                diag = INV[c, p - 1, here, :] + w
-                r = L[c, p - 1, here, :] + w * U[c, q, there, :] - diag * U[c, p, there, :]
-                inv = relaxation / diag
-                INV[c, p - 1, here, :] = inv
-                F[c, p, there, :] = r * inv
-                R[c, (p - 1) // 2, here, :] = R[c, (p - 1) // 2, here, :] + r
-
-    f_up = remote(F.at[:, X, rows], F.at[:, 0, rows], 7, up)
-    f_down = remote(F.at[:, 1, rows], F.at[:, X + 1, rows], 8, down)
-
-    @pl.when(has_up)
-    def _():
-        f_up.start()
-
-    @pl.when(has_down)
-    def _():
-        f_down.start()
+        outer_face(p_near, q_near, pl.multiple_of(i * 8, 8), None)
+
+    f_near = remote(F.at[:, p_near, rows], F.at[:, X + 1 - q_near, rows], base + 4, near)
+    f_near.start()
+    f_far = []
+    for n in range(PARTS):
+        @pl.when(has_far)
+        def _():
+            for copy in far1[n]:
+                copy.wait_recv()
+
+        @pl.loop(0, part // 8)
+        def _(i):
+            outer_face(p_far, q_far, pl.multiple_of(n * part + i * 8, 8), has_far)
+
+        there = pl.ds(OFF + n * part, part)
+        f_far.append(remote(F.at[:, p_far, there], F.at[:, X + 1 - q_far, there], base + 5 + n, far))
+
+        @pl.when(has_far)
+        def _():
+            f_far[n].start()
+
+    base = base + 5 + PARTS
 
     Y2, Y3 = Y // 2, Y // 4
     shape2, shape3 = (Y2, Z), (Y3, Z)
@@ -333,7 +343,7 @@
     half = Y2 // 2
     odd_half = odd2[:half]
     quad8 = quad[:8]
-    for side, p2 in ((0, 2), (1, 1)):
+    for side, p2 in ((0, 2 - odd), (1, 1 + odd)):
         for c in range(3):
             a = F2[c, p2, pl.ds(OFF, half), :]
             b = F2[c, p2, pl.ds(OFF + half, half), :]
@@ -342,16 +352,14 @@
             for q in range(1, 4):
                 v = jnp.where(quad8 == q, F3[c, 1, pl.ds(OFF + 8 * q, 8), :], v)
             PS[side, pl.ds(3 * half + 8 * c, 8), :] = v
-    c_up = remote(PS.at[0], PR.at[0], 9, up)
-    c_down = remote(PS.at[1], PR.at[1], 10, down)
-
-    @pl.when(has_up)
+    c_near = remote(PS.at[0], PR.at[0], base, near)
+    c_far = remote(PS.at[1], PR.at[1], base + 1, far)
+
+    @pl.when(has_far)
     def _():
-        c_up.start()
-
-    @pl.when(has_down)
-    def _():
-        c_down.start()
+        c_far.start()
+
+    c_near.start()
 
     own2 = jnp.where(sec == 0, OFF + Y2 - 1, OFF)
     own3 = jnp.where(sec == 0, OFF + Y3 - 1, OFF)
@@ -372,15 +380,10 @@
         S2[pl.ds(r, 1), :] = V[c, p, pl.ds(own, 1), :]
     for r in range(21, 24):
         S2[pl.ds(r, 1), :] = zero_row
-    cross2 = remote(S2, S2R, 11, across)
+    cross2 = remote(S2, S2R, base + 2, across)
     cross2.start()
-    cross2.wait()
-    for r, (V, c, p, own, halo) in enumerate(face_rows):
-        V[c, p, pl.ds(halo, 1), :] = S2R[pl.ds(r, 1), :]
-
-    @pl.loop(0, Y // 8)
-    def _(i):
-        y = pl.multiple_of(i * 8, 8)
+
+    def inner_sweep(y):
         here = pl.ds(y, 8)
         for p in range(1, X + 1):
             w = weights(p, y)
@@ -388,17 +391,49 @@
                 total, v = neighbours(F, c, p, y, w)
                 E[c, p - 1, here, :] = (4.0 / 3.0) * v + INV[c, p - 1, here, :] * total
 
-    @pl.when(has_down)
+    def outer_sweep(p, q, y):
+        here, there = pl.ds(y, 8), pl.ds(OFF + y, 8)
+        s = H[q, there, :] + H[p, there, :]
+        t = K[q, there, :] + K[p, there, :]
+        for c in range(3):
+            w = t if c == 0 else s
+            E[c, p - 1, here, :] = E[c, p - 1, here, :] + INV[c, p - 1, here, :] * (w * F[c, q, there, :])
+
+    f_near.wait_recv()
+
+    @pl.loop(0, Y // 8 - 1)
+    def _(i):
+        y = pl.multiple_of((i + sec) * 8, 8)
+        inner_sweep(y)
+        outer_sweep(p_near, q_near, y)
+
+    for n in range(PARTS):
+        @pl.when(has_far)
+        def _():
+            f_far[n].wait_recv()
+
+        @pl.loop(0, part // 8)
+        def _(i):
+            y = pl.multiple_of(n * part + i * 8, 8)
+
+            @pl.when(y != halo_chunk)
+            def _():
+                outer_sweep(p_far, q_far, y)
+
+    cross2.wait()
+    for r, (V, c, p, own, halo) in enumerate(face_rows):
+        V[c, p, pl.ds(halo, 1), :] = S2R[pl.ds(r, 1), :]
+    inner_sweep(halo_chunk)
+    outer_sweep(p_near, q_near, halo_chunk)
+    outer_sweep(p_far, q_far, halo_chunk)
+
+    c_near.wait_recv()
+
+    @pl.when(has_far)
     def _():
-        f_up.wait_recv()
-        c_up.wait_recv()
-
-    @pl.when(has_up)
-    def _():
-        f_down.wait_recv()
-        c_down.wait_recv()
-
-    for side, p2, p3, present in ((0, 0, 0, has_down), (1, 3, 2, has_up)):
+        c_far.wait_recv()
+
+    for side, p2, p3, present in ((0, 3 * (1 - odd), 2 * (1 - odd), True), (1, 3 * odd, 2 * odd, has_far)):
         for c in range(3):
             v = jnp.where(present, PR[side, pl.ds(half * c, half), :], 0.0)
             F2[c, p2, pl.ds(OFF, half), :] = jnp.where(odd_half, roll(v, 1), v)
@@ -436,26 +471,16 @@
     def _(i):
         y = pl.multiple_of(i * 8, 8)
         here = pl.ds(y, 8)
-        there = pl.ds(OFF + y, 8)
-        for p, q in ((1, 0), (2, None), (3, None), (4, X + 1)):
-            if q is not None:
-                s = H[q, there, :] + H[p, there, :]
-                t = K[q, there, :] + K[p, there, :]
+        for p in range(X):
             for c in range(3):
-                value = E[c, p - 1, here, :] + R[c, (p - 1) // 2, here, :]
-                if q is not None:
-                    w = t if c == 0 else s
-                    value = value + INV[c, p - 1, here, :] * (w * F[c, q, there, :])
-                out[c, p - 1, here, :] = value
-
-    @pl.when(has_up)
+                out[c, p, here, :] = E[c, p, here, :] + R[c, p // 2, here, :]
+
+    for copy in near1 + [f_near, c_near]:
+        copy.wait_send()
+
+    @pl.when(has_far)
     def _():
-        for copy in ups + [f_up, c_up]:
-            copy.wait_send()
-
-    @pl.when(has_down)
-    def _():
-        for copy in downs + [f_down, c_down]:
+        for copy in [copy for copies in far1 for copy in copies] + f_far + [c_far]:
             copy.wait_send()
 
 
@@ -465,7 +490,7 @@
     return pl.pallas_call(
         functools.partial(kernel, tiles),
         out_shape=jax.ShapeDtypeStruct(load_field.shape, f32),
-        in_specs=[pl.BlockSpec(memory_space=pl.ANY)] * 4,
+        in_specs=[pl.BlockSpec(memory_space=pltpu.HBM)] * 4,
         out_specs=pl.BlockSpec(memory_space=pltpu.VMEM),
         scratch_shapes=[
             pltpu.VMEM((3, X + 2, padded, Z), f32),
@@ -490,12 +515,12 @@
             pltpu.VMEM((3, 3, Y // 4 + 2 * OFF, Z), f32),
             pltpu.VMEM((3, 2, Y // 2, Z), f32),
             pltpu.SemaphoreType.DMA((4,)),
-            pltpu.SemaphoreType.DMA((12,)),
-            pltpu.SemaphoreType.DMA((12,)),
+            pltpu.SemaphoreType.DMA((4 * PARTS + 8,)),
+            pltpu.SemaphoreType.DMA((4 * PARTS + 8,)),
         ],
         compiler_params=pltpu.CompilerParams(
             collective_id=0, has_side_effects=True, vmem_limit_bytes=48 * 1024 * 1024),
-    )(load_field, iterate, phase_label, damage)
+    )(*[pltpu.with_memory_space_constraint(a, pltpu.HBM) for a in (load_field, iterate, phase_label, damage)])
 
 
 def solution(mesh):

time: 30.5 us -> 22.2 us (0.73)
  the two profiles are of different devices: /device:TPU:1 before, /device:TPU:153 now
where the time goes in v2:
time: 22.2 us; the launch traced here: 22.1 us
  Pallas kernels  21.2 us (95%)
  local copies, waits for them, and re-layouts  0.88 us (4%)
    pallas_call x1, Pallas kernels, per_device(): pl.pallas_call(functools.partial(kernel, tiles), out_shape=jax.ShapeDtype...  21.2 us
    unnamed x1, local copies, waits for them, and re-layouts  0.88 us

profile of v2, /device:TPU:153, one launch (start us, length us, event | category | flops | bytes accessed | tf_op | source)
XLA Modules:
  0.0 22.1 jit_solution(9225267612295516008)
XLA Ops:
  0.0 21.2 %shard_map.46 = f32[3,4,128,128]{3,2,1,0:T(8,128)S(1)} custom-call(f32[3,4,128,128]{3,2,1,0:T(8,128)} %load_hbm.1, f32[3,4,128,128]{3,2,1,0:T(8,128)} %u_hbm.1, s32[4,128,128]{2,1,0:T(8,128)} %lab_hbm.1, s32[4,128,128]{2,1,0:T(8,128)} %dam_hbm.1), custom_call_target="tpu_custom_call" | custom-call | tf_op jit(solution)/shard_map/pallas_call | solution.py:490
  21.2 0.9 %copy.6 = f32[3,4,128,128]{3,2,1,0:T(8,128)} copy(f32[3,4,128,128]{3,2,1,0:T(8,128)S(1)} %shard_map.46) | data formatting | bytes 1572864

commit v3 on v2

--- a/solution.py
+++ b/solution.py
@@ -53,7 +53,7 @@
 
 
 def kernel(tiles, load_hbm, u_hbm, lab_hbm, dam_hbm, out, U, F, L, INV, R, E, H, K, LAB, DAM, S1, S1R, S2, S2R,
-           PS, PR, W2, F2, I2, F3, EX, local_sem, send_sem, recv_sem):
+           PN, QN, PF, QF, W2, F2, I2, W3, F3, I3, EX, local_sem, send_sem, recv_sem):
     me = lax.axis_index("tile")
     sec = lax.axis_index("sec")
     odd = lax.rem(me, 2)
@@ -108,28 +108,40 @@
 
     rows = pl.ds(OFF, Y)
     part = Y // PARTS
-    far1 = []
-    for n in range(PARTS):
-        here, there = pl.ds(n * part, part), pl.ds(OFF + n * part, part)
-        far1.append([
-            remote(lab_hbm.at[p_far - 1, here], LAB.at[X + 1 - q_far, here], 3 * n, far),
-            remote(dam_hbm.at[p_far - 1, here], DAM.at[X + 1 - q_far, here], 3 * n + 1, far),
-            remote(u_hbm.at[:, p_far - 1, here], U.at[:, X + 1 - q_far, there], 3 * n + 2, far),
-        ])
-    base = 3 * PARTS
+    base = 5 * PARTS
+
+    def part_of(k):
+        n = k + (1 - sec) * (PARTS - 1 - 2 * k)
+        return pl.multiple_of(n * part, part)
+
+    def far1(k):
+        y = part_of(k)
+        here, there = pl.ds(y, part), pl.ds(OFF + y, part)
+        return [
+            remote(lab_hbm.at[p_far - 1, here], LAB.at[X + 1 - q_far, here], 3 * k, far),
+            remote(dam_hbm.at[p_far - 1, here], DAM.at[X + 1 - q_far, here], 3 * k + 1, far),
+            remote(u_hbm.at[:, p_far - 1, here], U.at[:, X + 1 - q_far, there], 3 * k + 2, far),
+        ]
+
+    def f_far(k):
+        there = pl.ds(OFF + part_of(k), part)
+        return remote(F.at[:, p_far, there], F.at[:, X + 1 - q_far, there], 3 * PARTS + k, far)
+
+    def c_far(k):
+        return remote(PF.at[k], QF.at[k], 4 * PARTS + k, far)
+
     near1 = [
         remote(lab_hbm.at[p_near - 1], LAB.at[X + 1 - q_near], base, near),
         remote(dam_hbm.at[p_near - 1], DAM.at[X + 1 - q_near], base + 1, near),
         remote(u_hbm.at[:, p_near - 1], U.at[:, X + 1 - q_near, rows], base + 2, near),
     ]
-
     cross1 = remote(S1, S1R, base + 3, across)
     cross1.start()
 
     @pl.when(has_far)
     def _():
-        for copies in far1:
-            for copy in copies:
+        for k in range(PARTS):
+            for copy in far1(k):
                 copy.start()
 
     for copy in near1:
@@ -252,114 +264,90 @@
 
     f_near = remote(F.at[:, p_near, rows], F.at[:, X + 1 - q_near, rows], base + 4, near)
     f_near.start()
-    f_far = []
-    for n in range(PARTS):
-        @pl.when(has_far)
-        def _():
-            for copy in far1[n]:
-                copy.wait_recv()
-
-        @pl.loop(0, part // 8)
-        def _(i):
-            outer_face(p_far, q_far, pl.multiple_of(n * part + i * 8, 8), has_far)
-
-        there = pl.ds(OFF + n * part, part)
-        f_far.append(remote(F.at[:, p_far, there], F.at[:, X + 1 - q_far, there], base + 5 + n, far))
-
-        @pl.when(has_far)
-        def _():
-            f_far[n].start()
-
-    base = base + 5 + PARTS
 
     Y2, Y3 = Y // 2, Y // 4
-    shape2, shape3 = (Y2, Z), (Y3, Z)
+    part2, part3 = part // 2, part // 4
+    shape2, shape3 = (part2, Z), (part3, Z)
     odd2 = (lanes(shape2) & 1) == 1
+    quad = lanes(shape3) & 3
+    high3 = quad >= 2
+    j_near, j_far = 1 - odd, odd
 
     def pairs(v):
         return v + jnp.where(odd2, roll(v, 1), roll(v, -1))
 
-    def every_other(M, p, first):
-        return M[p, pl.ds(first, Y2, stride=2), :]
-
-    for m, M in enumerate((H, K)):
-        for j in range(3):
-            face = every_other(M, 2 * j, OFF) + every_other(M, 2 * j, OFF + 1)
-            face = face + every_other(M, 2 * j + 1, OFF) + every_other(M, 2 * j + 1, OFF + 1)
-            W2[m, j] = pairs(face)
-        for j in range(2):
-            r7, r8, r9, r10 = [
-                every_other(M, 1 + 2 * j, OFF + d) + every_other(M, 2 + 2 * j, OFF + d) for d in (-1, 0, 1, 2)]
-            W2[m, 3 + j] = pairs(r7 + r8)
-            W2[m, 5 + j] = pairs(r9 + r10)
-            cell = r8 + r9
-            low = cell + from_below(cell, 1)
-            high = cell + from_above(cell, 1)
-            W2[m, 7 + j] = jnp.where(odd2, roll(low, 1), low)
-            W2[m, 9 + j] = jnp.where(odd2, high, roll(high, -1))
+    def quads(v):
+        return v + jnp.where(high3, roll(v, 2), roll(v, -2))
+
+    def fine_rows(M, p, first):
+        return M[p, pl.ds(first, part2, stride=2), :]
+
+    def coarse_rows(m, slot, y2, first):
+        return W2[m, slot, pl.ds(y2 + first, part3, stride=2), :]
 
     def kinds(c):
         return [1 if c == a else 0 for a in range(3)]
 
-    for c in range(3):
-        kx, ky, kz = kinds(c)
-        for j in range(2):
-            diag = W2[kx, j] + W2[kx, j + 1] + W2[ky, 3 + j] + W2[ky, 5 + j] + W2[kz, 7 + j] + W2[kz, 9 + j]
-            inv = relaxation / diag
-            I2[c, j] = inv
-            res = R[c, j, pl.ds(0, Y2, stride=2), :] + R[c, j, pl.ds(1, Y2, stride=2), :]
-            res = pairs(res)
-            EX[c, j] = res
-            F2[c, 1 + j, pl.ds(OFF, Y2), :] = res * inv
-
-    quad = lanes(shape3) & 3
-    high3 = quad >= 2
-
-    def quads(v):
-        return v + jnp.where(high3, roll(v, 2), roll(v, -2))
-
-    def row_of(m, slot, first):
-        return W2[m, slot, pl.ds(first, Y3, stride=2), :]
-
-    w3 = {}
-    for m in range(2):
-        w3[m, "xl"] = quads(row_of(m, 0, 0) + row_of(m, 0, 1))
-        w3[m, "xu"] = quads(row_of(m, 2, 0) + row_of(m, 2, 1))
-        w3[m, "yl"] = quads(row_of(m, 3, 0) + row_of(m, 4, 0))
-        w3[m, "yu"] = quads(row_of(m, 5, 1) + row_of(m, 6, 1))
-        low = row_of(m, 7, 0) + row_of(m, 7, 1) + row_of(m, 8, 0) + row_of(m, 8, 1)
-        high = row_of(m, 9, 0) + row_of(m, 9, 1) + row_of(m, 10, 0) + row_of(m, 10, 1)
-        w3[m, "zl"] = jnp.where(high3, roll(low, 2), low)
-        w3[m, "zu"] = jnp.where(high3, high, roll(high, -2))
-    inv3 = []
-    for c in range(3):
-        kx, ky, kz = kinds(c)
-        diag = w3[kx, "xl"] + w3[kx, "xu"] + w3[ky, "yl"] + w3[ky, "yu"] + w3[kz, "zl"] + w3[kz, "zu"]
-        inv3.append(relaxation / diag)
-        res = EX[c, 0, pl.ds(0, Y3, stride=2), :] + EX[c, 0, pl.ds(1, Y3, stride=2), :]
-        res = res + EX[c, 1, pl.ds(0, Y3, stride=2), :] + EX[c, 1, pl.ds(1, Y3, stride=2), :]
-        F3[c, 1, pl.ds(OFF, Y3), :] = quads(res) * inv3[c]
-
-    half = Y2 // 2
+    def x_face(M, p, q, y):
+        face = fine_rows(M, p, OFF + y) + fine_rows(M, p, OFF + y + 1)
+        return pairs(face + fine_rows(M, q, OFF + y) + fine_rows(M, q, OFF + y + 1))
+
+    def residual_two(c, j, y):
+        return pairs(fine_rows(R.at[c], j, y) + fine_rows(R.at[c], j, y + 1))
+
+    @pl.loop(0, PARTS)
+    def _(n):
+        y = pl.multiple_of(n * part, part)
+        y2 = pl.multiple_of(n * part2, part2)
+        y3 = pl.multiple_of(n * part3, part3)
+        at2, at3 = pl.ds(y2, part2), pl.ds(y3, part3)
+        sides = {}
+        for m, M in enumerate((H, K)):
+            mid = x_face(M, 2, 3, y)
+            close = x_face(M, p_near, q_near, y)
+            W2[m, 1, at2, :] = mid
+            W2[m, 2 - 2 * odd, at2, :] = close
+            W3[m, 1 - odd, at3, :] = quads(
+                coarse_rows(m, 2 - 2 * odd, y2, 0) + coarse_rows(m, 2 - 2 * odd, y2, 1))
+            for j in range(2):
+                r7, r8, r9, r10 = [
+                    fine_rows(M, 1 + 2 * j, OFF + y + d) + fine_rows(M, 2 + 2 * j, OFF + y + d) for d in (-1, 0, 1, 2)]
+                yl, yu = pairs(r7 + r8), pairs(r9 + r10)
+                cell = r8 + r9
+                low = cell + from_below(cell, 1)
+                high = cell + from_above(cell, 1)
+                zl = jnp.where(odd2, roll(low, 1), low)
+                zu = jnp.where(odd2, high, roll(high, -1))
+                for slot, value in ((3, yl), (5, yu), (7, zl), (9, zu)):
+                    W2[m, slot + j, at2, :] = value
+                sides[m, j, 0] = mid
+                sides[m, j, 1] = yl + yu
+                sides[m, j, 2] = zl + zu
+            W3[m, 2, at3, :] = quads(coarse_rows(m, 3, y2, 0) + coarse_rows(m, 4, y2, 0))
+            W3[m, 3, at3, :] = quads(coarse_rows(m, 5, y2, 1) + coarse_rows(m, 6, y2, 1))
+            low = coarse_rows(m, 7, y2, 0) + coarse_rows(m, 7, y2, 1)
+            low = low + coarse_rows(m, 8, y2, 0) + coarse_rows(m, 8, y2, 1)
+            high = coarse_rows(m, 9, y2, 0) + coarse_rows(m, 9, y2, 1)
+            high = high + coarse_rows(m, 10, y2, 0) + coarse_rows(m, 10, y2, 1)
+            W3[m, 4, at3, :] = jnp.where(high3, roll(low, 2), low)
+            W3[m, 5, at3, :] = jnp.where(high3, high, roll(high, -2))
+        for c in range(3):
+            kx, ky, kz = kinds(c)
+            for j in range(2):
+                I2[c, j, at2, :] = sides[kx, j, 0] + sides[ky, j, 1] + sides[kz, j, 2]
+            inv = relaxation / (I2[c, j_near, at2, :] + W2[kx, 2 - 2 * odd, at2, :])
+            I2[c, j_near, at2, :] = inv
+            res = residual_two(c, j_near, y)
+            EX[c, j_near, at2, :] = res
+            F2[c, 1 + j_near, pl.ds(OFF + y2, part2), :] = res * inv
+            I3[c, at3, :] = (W3[kx, 1 - odd, at3, :] + W3[ky, 2, at3, :] + W3[ky, 3, at3, :]
+                             + W3[kz, 4, at3, :] + W3[kz, 5, at3, :])
+
+    half = part2 // 2
     odd_half = odd2[:half]
-    quad8 = quad[:8]
-    for side, p2 in ((0, 2 - odd), (1, 1 + odd)):
-        for c in range(3):
-            a = F2[c, p2, pl.ds(OFF, half), :]
-            b = F2[c, p2, pl.ds(OFF + half, half), :]
-            PS[side, pl.ds(half * c, half), :] = jnp.where(odd_half, b, a)
-            v = F3[c, 1, pl.ds(OFF, 8), :]
-            for q in range(1, 4):
-                v = jnp.where(quad8 == q, F3[c, 1, pl.ds(OFF + 8 * q, 8), :], v)
-            PS[side, pl.ds(3 * half + 8 * c, 8), :] = v
-    c_near = remote(PS.at[0], PR.at[0], base, near)
-    c_far = remote(PS.at[1], PR.at[1], base + 1, far)
-
-    @pl.when(has_far)
-    def _():
-        c_far.start()
-
-    c_near.start()
+
+    def packed(V, c, p, y2):
+        return jnp.where(odd_half, V[c, p, pl.ds(OFF + y2 + half, half), :], V[c, p, pl.ds(OFF + y2, half), :])
 
     own2 = jnp.where(sec == 0, OFF + Y2 - 1, OFF)
     own3 = jnp.where(sec == 0, OFF + Y3 - 1, OFF)
@@ -376,12 +364,63 @@
             F2[c, p, pl.ds(edge2, 1), :] = zero_row
         face_rows.append((F3, c, 1, own3, halo3))
         F3[c, 1, pl.ds(edge3, 1), :] = zero_row
-    for r, (V, c, p, own, halo) in enumerate(face_rows):
-        S2[pl.ds(r, 1), :] = V[c, p, pl.ds(own, 1), :]
     for r in range(21, 24):
         S2[pl.ds(r, 1), :] = zero_row
-    cross2 = remote(S2, S2R, base + 2, across)
-    cross2.start()
+    cross2 = remote(S2, S2R, base + 5, across)
+
+    @pl.loop(0, PARTS)
+    def _(k):
+        y = part_of(k)
+
+        @pl.when(has_far)
+        def _():
+            for copy in far1(k):
+                copy.wait_recv()
+
+        for i in range(part // 8):
+            outer_face(p_far, q_far, pl.multiple_of(y + i * 8, 8), has_far)
+
+        @pl.when(has_far)
+        def _():
+            f_far(k).start()
+
+        y2, y3 = pl.multiple_of(y // 2, part2), pl.multiple_of(y // 4, part3)
+        at2, at3 = pl.ds(y2, part2), pl.ds(y3, part3)
+        for m, M in enumerate((H, K)):
+            W2[m, 2 * odd, at2, :] = x_face(M, p_far, q_far, y)
+            W3[m, odd, at3, :] = quads(coarse_rows(m, 2 * odd, y2, 0) + coarse_rows(m, 2 * odd, y2, 1))
+        deep = jnp.zeros(shape3, jnp.float32)
+        for c in range(3):
+            kx = kinds(c)[0]
+            inv = relaxation / (I2[c, j_far, at2, :] + W2[kx, 2 * odd, at2, :])
+            I2[c, j_far, at2, :] = inv
+            res = residual_two(c, j_far, y)
+            EX[c, j_far, at2, :] = res
+            F2[c, 1 + j_far, pl.ds(OFF + y2, part2), :] = res * inv
+            inv = relaxation / (I3[c, at3, :] + W3[kx, odd, at3, :])
+            I3[c, at3, :] = inv
+            res = EX[c, 0, pl.ds(y2, part3, stride=2), :] + EX[c, 0, pl.ds(y2 + 1, part3, stride=2), :]
+            res = res + EX[c, 1, pl.ds(y2, part3, stride=2), :] + EX[c, 1, pl.ds(y2 + 1, part3, stride=2), :]
+            first = quads(res) * inv
+            F3[c, 1, pl.ds(OFF + y3, part3), :] = first
+            deep = jnp.where(quad == c, first, deep)
+            PF[k, pl.ds(half * c, half), :] = packed(F2, c, 1 + j_far, y2)
+            PN[k, pl.ds(half * c, half), :] = packed(F2, c, 1 + j_near, y2)
+        PF[k, pl.ds(3 * half, part3), :] = deep
+        PN[k, pl.ds(3 * half, part3), :] = deep
+
+        @pl.when(has_far)
+        def _():
+            c_far(k).start()
+
+        @pl.when(k == 0)
+        def _():
+            for r, (V, c, p, own, halo) in enumerate(face_rows):
+                S2[pl.ds(r, 1), :] = V[c, p, pl.ds(own, 1), :]
+            cross2.start()
+
+    c_near = remote(PN, QN, base + 6, near)
+    c_near.start()
 
     def inner_sweep(y):
         here = pl.ds(y, 8)
@@ -407,81 +446,94 @@
         inner_sweep(y)
         outer_sweep(p_near, q_near, y)
 
-    for n in range(PARTS):
-        @pl.when(has_far)
-        def _():
-            f_far[n].wait_recv()
-
-        @pl.loop(0, part // 8)
-        def _(i):
-            y = pl.multiple_of(n * part + i * 8, 8)
-
-            @pl.when(y != halo_chunk)
-            def _():
-                outer_sweep(p_far, q_far, y)
-
     cross2.wait()
     for r, (V, c, p, own, halo) in enumerate(face_rows):
         V[c, p, pl.ds(halo, 1), :] = S2R[pl.ds(r, 1), :]
     inner_sweep(halo_chunk)
     outer_sweep(p_near, q_near, halo_chunk)
-    outer_sweep(p_far, q_far, halo_chunk)
+
+    def unpack(Q, k, q2, q3, present):
+        y = part_of(k)
+        y2, y3 = y // 2, y // 4
+        for c in range(3):
+            v = Q[k, pl.ds(half * c, half), :]
+            if present is not None:
+                v = jnp.where(present, v, 0.0)
+            F2[c, q2, pl.ds(OFF + y2, half), :] = jnp.where(odd_half, roll(v, 1), v)
+            F2[c, q2, pl.ds(OFF + y2 + half, half), :] = jnp.where(odd_half, v, roll(v, -1))
+        v = Q[k, pl.ds(3 * half, part3), :]
+        if present is not None:
+            v = jnp.where(present, v, 0.0)
+        for c in range(3):
+            spread = v
+            for lane in range(4):
+                if lane != c:
+                    spread = jnp.where(quad == lane, roll(v, lane - c), spread)
+            F3[c, q3, pl.ds(OFF + y3, part3), :] = spread
 
     c_near.wait_recv()
+    for k in range(PARTS):
+        unpack(QN, k, 3 * (1 - odd), 2 * (1 - odd), None)
+
+    @pl.loop(0, PARTS)
+    def _(k):
+        y = part_of(k)
+        y2, y3 = pl.multiple_of(y // 2, part2), pl.multiple_of(y // 4, part3)
+        at2, at3 = pl.ds(y2, part2), pl.ds(y3, part3)
+
+        @pl.when(has_far)
+        def _():
+            f_far(k).wait_recv()
+
+        for i in range(part // 8):
+            outer_sweep(p_far, q_far, pl.multiple_of(y + i * 8, 8))
+
+        @pl.when(has_far)
+        def _():
+            c_far(k).wait_recv()
+
+        unpack(QF, k, 3 * odd, 2 * odd, has_far)
+        for c in range(3):
+            kx, ky, kz = kinds(c)
+
+            def f3(p, d):
+                return F3[c, p, pl.ds(OFF + y3 + d, part3), :]
+
+            v = f3(1, 0)
+            total = W3[kx, 0, at3, :] * f3(0, 0) + W3[kx, 1, at3, :] * f3(2, 0)
+            total = total + W3[ky, 2, at3, :] * f3(1, -1) + W3[ky, 3, at3, :] * f3(1, 1)
+            total = total + W3[kz, 4, at3, :] * from_below(v, 4) + W3[kz, 5, at3, :] * from_above(v, 4)
+            e3 = (4.0 / 3.0) * v + I3[c, at3, :] * total
+            EX[c, 0, pl.ds(y2, part3, stride=2), :] = e3
+            EX[c, 0, pl.ds(y2 + 1, part3, stride=2), :] = e3
+            e3 = EX[c, 0, at2, :]
+
+            def f2(p, d):
+                return F2[c, p, pl.ds(OFF + y2 + d, part2), :]
+
+            for j in range(2):
+                p = 1 + j
+                v = f2(p, 0)
+                total = W2[kx, j, at2, :] * f2(p - 1, 0) + W2[kx, j + 1, at2, :] * f2(p + 1, 0)
+                total = total + W2[ky, 3 + j, at2, :] * f2(p, -1) + W2[ky, 5 + j, at2, :] * f2(p, 1)
+                total = total + W2[kz, 7 + j, at2, :] * from_below(v, 2) + W2[kz, 9 + j, at2, :] * from_above(v, 2)
+                e2 = (4.0 / 3.0) * v + I2[c, j, at2, :] * total + e3
+                R[c, j, pl.ds(y, part2, stride=2), :] = e2
+                R[c, j, pl.ds(y + 1, part2, stride=2), :] = e2
+        for i in range(part // 8):
+            here = pl.ds(pl.multiple_of(y + i * 8, 8), 8)
+            for p in range(X):
+                for c in range(3):
+                    out[c, p, here, :] = E[c, p, here, :] + R[c, p // 2, here, :]
+
+    for copy in near1 + [f_near, c_near]:
+        copy.wait_send()
 
     @pl.when(has_far)
     def _():
-        c_far.wait_recv()
-
-    for side, p2, p3, present in ((0, 3 * (1 - odd), 2 * (1 - odd), True), (1, 3 * odd, 2 * odd, has_far)):
-        for c in range(3):
-            v = jnp.where(present, PR[side, pl.ds(half * c, half), :], 0.0)
-            F2[c, p2, pl.ds(OFF, half), :] = jnp.where(odd_half, roll(v, 1), v)
-            F2[c, p2, pl.ds(OFF + half, half), :] = jnp.where(odd_half, v, roll(v, -1))
-            v = jnp.where(present, PR[side, pl.ds(3 * half + 8 * c, 8), :], 0.0)
-            for q in range(4):
-                spread = v
-                for lane in range(4):
-                    if lane != q:
-                        spread = jnp.where(quad8 == lane, roll(v, lane - q), spread)
-                F3[c, p3, pl.ds(OFF + 8 * q, 8), :] = spread
-
-    for c in range(3):
-        kx, ky, kz = kinds(c)
-        v = F3[c, 1, pl.ds(OFF, Y3), :]
-        total = w3[kx, "xl"] * F3[c, 0, pl.ds(OFF, Y3), :] + w3[kx, "xu"] * F3[c, 2, pl.ds(OFF, Y3), :]
-        total = total + w3[ky, "yl"] * F3[c, 1, pl.ds(OFF - 1, Y3), :] + w3[ky, "yu"] * F3[c, 1, pl.ds(OFF + 1, Y3), :]
-        total = total + w3[kz, "zl"] * from_below(v, 4) + w3[kz, "zu"] * from_above(v, 4)
-        e3 = (4.0 / 3.0) * v + inv3[c] * total
-        EX[c, 0, pl.ds(0, Y3, stride=2), :] = e3
-        EX[c, 0, pl.ds(1, Y3, stride=2), :] = e3
-        e3 = EX[c, 0]
-        for j in range(2):
-            p = 1 + j
-            v = F2[c, p, pl.ds(OFF, Y2), :]
-            total = W2[kx, j] * F2[c, p - 1, pl.ds(OFF, Y2), :] + W2[kx, j + 1] * F2[c, p + 1, pl.ds(OFF, Y2), :]
-            total = total + W2[ky, 3 + j] * F2[c, p, pl.ds(OFF - 1, Y2), :]
-            total = total + W2[ky, 5 + j] * F2[c, p, pl.ds(OFF + 1, Y2), :]
-            total = total + W2[kz, 7 + j] * from_below(v, 2) + W2[kz, 9 + j] * from_above(v, 2)
-            e2 = (4.0 / 3.0) * v + I2[c, j] * total + e3
-            R[c, j, pl.ds(0, Y2, stride=2), :] = e2
-            R[c, j, pl.ds(1, Y2, stride=2), :] = e2
-
-    @pl.loop(0, Y // 8)
-    def _(i):
-        y = pl.multiple_of(i * 8, 8)
-        here = pl.ds(y, 8)
-        for p in range(X):
-            for c in range(3):
-                out[c, p, here, :] = E[c, p, here, :] + R[c, p // 2, here, :]
-
-    for copy in near1 + [f_near, c_near]:
-        copy.wait_send()
-
-    @pl.when(has_far)
-    def _():
-        for copy in [copy for copies in far1 for copy in copies] + f_far + [c_far]:
-            copy.wait_send()
+        for k in range(PARTS):
+            for copy in far1(k) + [f_far(k), c_far(k)]:
+                copy.wait_send()
 
 
 def per_device(tiles, load_field, iterate, phase_label, damage):
@@ -507,16 +559,20 @@
             pltpu.VMEM((24, Z), f32),
             pltpu.VMEM((24, Z), f32),
             pltpu.VMEM((24, Z), f32),
-            pltpu.VMEM((2, 120, Z), f32),
-            pltpu.VMEM((2, 120, Z), f32),
+            pltpu.VMEM((PARTS, Y // PARTS, Z), f32),
+            pltpu.VMEM((PARTS, Y // PARTS, Z), f32),
+            pltpu.VMEM((PARTS, Y // PARTS, Z), f32),
+            pltpu.VMEM((PARTS, Y // PARTS, Z), f32),
             pltpu.VMEM((2, 11, Y // 2, Z), f32),
             pltpu.VMEM((3, 4, Y // 2 + 2 * OFF, Z), f32),
             pltpu.VMEM((3, 2, Y // 2, Z), f32),
+            pltpu.VMEM((2, 6, Y // 4, Z), f32),
             pltpu.VMEM((3, 3, Y // 4 + 2 * OFF, Z), f32),
+            pltpu.VMEM((3, Y // 4, Z), f32),
             pltpu.VMEM((3, 2, Y // 2, Z), f32),
             pltpu.SemaphoreType.DMA((4,)),
-            pltpu.SemaphoreType.DMA((4 * PARTS + 8,)),
-            pltpu.SemaphoreType.DMA((4 * PARTS + 8,)),
+            pltpu.SemaphoreType.DMA((5 * PARTS + 7,)),
+            pltpu.SemaphoreType.DMA((5 * PARTS + 7,)),
         ],
         compiler_params=pltpu.CompilerParams(
             collective_id=0, has_side_effects=True, vmem_limit_bytes=48 * 1024 * 1024),

time: 22.2 us -> 20.2 us (0.910)
  the two profiles are of different devices: /device:TPU:153 before, /device:TPU:3 now
where the time goes in v3:
time: 20.2 us; the launch traced here: 19.9 us
  Pallas kernels  19 us (94%)
  local copies, waits for them, and re-layouts  0.88 us (4%)
    pallas_call x1, Pallas kernels, per_device(): pl.pallas_call(functools.partial(kernel, tiles), out_shape=jax.ShapeDtype...  19 us
    unnamed x1, local copies, waits for them, and re-layouts  0.88 us

profile of v3, /device:TPU:3, one launch (start us, length us, event | category | flops | bytes accessed | tf_op | source)
XLA Modules:
  0.0 19.9 jit_solution(5169776098603718198)
XLA Ops:
  0.0 19.0 %shard_map.46 = f32[3,4,128,128]{3,2,1,0:T(8,128)S(1)} custom-call(f32[3,4,128,128]{3,2,1,0:T(8,128)} %load_hbm.1, f32[3,4,128,128]{3,2,1,0:T(8,128)} %u_hbm.1, s32[4,128,128]{2,1,0:T(8,128)} %lab_hbm.1, s32[4,128,128]{2,1,0:T(8,128)} %dam_hbm.1), custom_call_target="tpu_custom_call" | custom-call | tf_op jit(solution)/shard_map/pallas_call | solution.py:542
  19.0 0.9 %copy.6 = f32[3,4,128,128]{3,2,1,0:T(8,128)} copy(f32[3,4,128,128]{3,2,1,0:T(8,128)S(1)} %shard_map.46) | data formatting | bytes 1572864

commit v4 on v3

--- a/solution.py
+++ b/solution.py
@@ -17,7 +17,7 @@
 X = 4
 Y = 128
 Z = 128
-PARTS = 4
+PARTS = 2
 OFF = 8
 
 
@@ -87,8 +87,6 @@
     edge_row = jnp.where(sec == 0, OFF - 1, OFF + Y)
     faces = [H.at[pl.ds(1, X)], K.at[pl.ds(1, X)]] + [U.at[c, pl.ds(1, X)] for c in range(3)]
     zero_row = jnp.zeros((1, Z), jnp.float32)
-    for r in range(20, 24):
-        S1[pl.ds(r, 1), :] = zero_row
     for copy in loads[:2]:
         copy.wait()
     for p in range(X):
@@ -355,17 +353,40 @@
     halo3 = jnp.where(sec == 0, OFF + Y3, OFF - 1)
     edge2 = jnp.where(sec == 0, OFF - 1, OFF + Y2)
     edge3 = jnp.where(sec == 0, OFF - 1, OFF + Y3)
-    face_rows = []
+    quad_row = lanes((1, Z)) & 3
+    odd_row = (quad_row & 1) == 1
+    fine_faces = [(c, p) for c in range(3) for p in range(1, X + 1)]
     for c in range(3):
-        for p in range(1, X + 1):
-            face_rows.append((F, c, p, own_row, halo_row))
-        for p in (1, 2):
-            face_rows.append((F2, c, p, own2, halo2))
-            F2[c, p, pl.ds(edge2, 1), :] = zero_row
-        face_rows.append((F3, c, 1, own3, halo3))
+        F2[c, 1, pl.ds(edge2, 1), :] = zero_row
+        F2[c, 2, pl.ds(edge2, 1), :] = zero_row
         F3[c, 1, pl.ds(edge3, 1), :] = zero_row
-    for r in range(21, 24):
-        S2[pl.ds(r, 1), :] = zero_row
+
+    def pack_rows():
+        for r, (c, p) in enumerate(fine_faces):
+            S2[pl.ds(r, 1), :] = F[c, p, pl.ds(own_row, 1), :]
+        deep = zero_row
+        for c in range(3):
+            S2[pl.ds(12 + c, 1), :] = jnp.where(odd_row, F2[c, 2, pl.ds(own2, 1), :], F2[c, 1, pl.ds(own2, 1), :])
+            deep = jnp.where(quad_row == c, F3[c, 1, pl.ds(own3, 1), :], deep)
+        S2[pl.ds(15, 1), :] = deep
+
+    def unpack_rows():
+        for r, (c, p) in enumerate(fine_faces):
+            F[c, p, pl.ds(halo_row, 1), :] = S2R[pl.ds(r, 1), :]
+        deep = S2R[pl.ds(15, 1), :]
+        for c in range(3):
+            v = S2R[pl.ds(12 + c, 1), :]
+            F2[c, 1, pl.ds(halo2, 1), :] = jnp.where(odd_row, roll(v, 1), v)
+            F2[c, 2, pl.ds(halo2, 1), :] = jnp.where(odd_row, v, roll(v, -1))
+            F3[c, 1, pl.ds(halo3, 1), :] = spread_quad(deep, c, quad_row)
+
+    def spread_quad(v, c, quad):
+        spread = v
+        for lane in range(4):
+            if lane != c:
+                spread = jnp.where(quad == lane, roll(v, lane - c), spread)
+        return spread
+
     cross2 = remote(S2, S2R, base + 5, across)
 
     @pl.loop(0, PARTS)
@@ -415,8 +436,7 @@
 
         @pl.when(k == 0)
         def _():
-            for r, (V, c, p, own, halo) in enumerate(face_rows):
-                S2[pl.ds(r, 1), :] = V[c, p, pl.ds(own, 1), :]
+            pack_rows()
             cross2.start()
 
     c_near = remote(PN, QN, base + 6, near)
@@ -447,8 +467,7 @@
         outer_sweep(p_near, q_near, y)
 
     cross2.wait()
-    for r, (V, c, p, own, halo) in enumerate(face_rows):
-        V[c, p, pl.ds(halo, 1), :] = S2R[pl.ds(r, 1), :]
+    unpack_rows()
     inner_sweep(halo_chunk)
     outer_sweep(p_near, q_near, halo_chunk)
 
@@ -465,11 +484,7 @@
         if present is not None:
             v = jnp.where(present, v, 0.0)
         for c in range(3):
-            spread = v
-            for lane in range(4):
-                if lane != c:
-                    spread = jnp.where(quad == lane, roll(v, lane - c), spread)
-            F3[c, q3, pl.ds(OFF + y3, part3), :] = spread
+            F3[c, q3, pl.ds(OFF + y3, part3), :] = spread_quad(v, c, quad)
 
     c_near.wait_recv()
     for k in range(PARTS):
@@ -555,10 +570,10 @@
             pltpu.VMEM((X + 2, padded, Z), f32),
             pltpu.VMEM((X + 2, Y, Z), i32),
             pltpu.VMEM((X + 2, Y, Z), i32),
-            pltpu.VMEM((24, Z), f32),
-            pltpu.VMEM((24, Z), f32),
-            pltpu.VMEM((24, Z), f32),
-            pltpu.VMEM((24, Z), f32),
+            pltpu.VMEM((20, Z), f32),
+            pltpu.VMEM((20, Z), f32),
+            pltpu.VMEM((16, Z), f32),
+            pltpu.VMEM((16, Z), f32),
             pltpu.VMEM((PARTS, Y // PARTS, Z), f32),
             pltpu.VMEM((PARTS, Y // PARTS, Z), f32),
             pltpu.VMEM((PARTS, Y // PARTS, Z), f32),

time: 20.2 us -> 19.7 us (0.975); the launches traced: 19.9 us -> 19.6 us
  Pallas kernels: 19 us -> 18.7 us
    pallas_call x1, Pallas kernels: 19 us -> 18.7 us  [per_device(): pl.pallas_call(functools.partial(kernel, tiles), out_shape=jax.ShapeDtype...]
where the time goes in v4:
time: 19.7 us; the launch traced here: 19.6 us
  Pallas kernels  18.7 us (95%)
  local copies, waits for them, and re-layouts  0.88 us (4%)
    pallas_call x1, Pallas kernels, per_device(): pl.pallas_call(functools.partial(kernel, tiles), out_shape=jax.ShapeDtype...  18.7 us
    unnamed x1, local copies, waits for them, and re-layouts  0.88 us

profile of v4, /device:TPU:3, one launch (start us, length us, event | category | flops | bytes accessed | tf_op | source)
XLA Modules:
  0.0 19.6 jit_solution(910403971417105137)
XLA Ops:
  0.0 18.7 %shard_map.46 = f32[3,4,128,128]{3,2,1,0:T(8,128)S(1)} custom-call(f32[3,4,128,128]{3,2,1,0:T(8,128)} %load_hbm.1, f32[3,4,128,128]{3,2,1,0:T(8,128)} %u_hbm.1, s32[4,128,128]{2,1,0:T(8,128)} %lab_hbm.1, s32[4,128,128]{2,1,0:T(8,128)} %dam_hbm.1), custom_call_target="tpu_custom_call" | custom-call | tf_op jit(solution)/shard_map/pallas_call | solution.py:557
  18.7 0.9 %copy.6 = f32[3,4,128,128]{3,2,1,0:T(8,128)} copy(f32[3,4,128,128]{3,2,1,0:T(8,128)S(1)} %shard_map.46) | data formatting | bytes 1572864

commit v5 on v4

--- a/solution.py
+++ b/solution.py
@@ -116,9 +116,9 @@
         y = part_of(k)
         here, there = pl.ds(y, part), pl.ds(OFF + y, part)
         return [
-            remote(lab_hbm.at[p_far - 1, here], LAB.at[X + 1 - q_far, here], 3 * k, far),
-            remote(dam_hbm.at[p_far - 1, here], DAM.at[X + 1 - q_far, here], 3 * k + 1, far),
-            remote(u_hbm.at[:, p_far - 1, here], U.at[:, X + 1 - q_far, there], 3 * k + 2, far),
+            remote(LAB.at[p_far, here], LAB.at[X + 1 - q_far, here], 3 * k, far),
+            remote(DAM.at[p_far, here], DAM.at[X + 1 - q_far, here], 3 * k + 1, far),
+            remote(U.at[:, p_far, there], U.at[:, X + 1 - q_far, there], 3 * k + 2, far),
         ]
 
     def f_far(k):
@@ -129,9 +129,9 @@
         return remote(PF.at[k], QF.at[k], 4 * PARTS + k, far)
 
     near1 = [
-        remote(lab_hbm.at[p_near - 1], LAB.at[X + 1 - q_near], base, near),
-        remote(dam_hbm.at[p_near - 1], DAM.at[X + 1 - q_near], base + 1, near),
-        remote(u_hbm.at[:, p_near - 1], U.at[:, X + 1 - q_near, rows], base + 2, near),
+        remote(LAB.at[p_near], LAB.at[X + 1 - q_near], base, near),
+        remote(DAM.at[p_near], DAM.at[X + 1 - q_near], base + 1, near),
+        remote(U.at[:, p_near, rows], U.at[:, X + 1 - q_near, rows], base + 2, near),
     ]
     cross1 = remote(S1, S1R, base + 3, across)
     cross1.start()
@@ -401,10 +401,6 @@
         for i in range(part // 8):
             outer_face(p_far, q_far, pl.multiple_of(y + i * 8, 8), has_far)
 
-        @pl.when(has_far)
-        def _():
-            f_far(k).start()
-
         y2, y3 = pl.multiple_of(y // 2, part2), pl.multiple_of(y // 4, part3)
         at2, at3 = pl.ds(y2, part2), pl.ds(y3, part3)
         for m, M in enumerate((H, K)):
@@ -433,6 +429,7 @@
         @pl.when(has_far)
         def _():
             c_far(k).start()
+            f_far(k).start()
 
         @pl.when(k == 0)
         def _():
@@ -450,13 +447,13 @@
                 total, v = neighbours(F, c, p, y, w)
                 E[c, p - 1, here, :] = (4.0 / 3.0) * v + INV[c, p - 1, here, :] * total
 
-    def outer_sweep(p, q, y):
+    def outer_sweep(target, p, q, y):
         here, there = pl.ds(y, 8), pl.ds(OFF + y, 8)
         s = H[q, there, :] + H[p, there, :]
         t = K[q, there, :] + K[p, there, :]
         for c in range(3):
             w = t if c == 0 else s
-            E[c, p - 1, here, :] = E[c, p - 1, here, :] + INV[c, p - 1, here, :] * (w * F[c, q, there, :])
+            target[c, p - 1, here, :] = target[c, p - 1, here, :] + INV[c, p - 1, here, :] * (w * F[c, q, there, :])
 
     f_near.wait_recv()
 
@@ -464,12 +461,12 @@
     def _(i):
         y = pl.multiple_of((i + sec) * 8, 8)
         inner_sweep(y)
-        outer_sweep(p_near, q_near, y)
+        outer_sweep(E, p_near, q_near, y)
 
     cross2.wait()
     unpack_rows()
     inner_sweep(halo_chunk)
-    outer_sweep(p_near, q_near, halo_chunk)
+    outer_sweep(E, p_near, q_near, halo_chunk)
 
     def unpack(Q, k, q2, q3, present):
         y = part_of(k)
@@ -495,13 +492,6 @@
         y = part_of(k)
         y2, y3 = pl.multiple_of(y // 2, part2), pl.multiple_of(y // 4, part3)
         at2, at3 = pl.ds(y2, part2), pl.ds(y3, part3)
-
-        @pl.when(has_far)
-        def _():
-            f_far(k).wait_recv()
-
-        for i in range(part // 8):
-            outer_sweep(p_far, q_far, pl.multiple_of(y + i * 8, 8))
 
         @pl.when(has_far)
         def _():
@@ -540,6 +530,13 @@
             for p in range(X):
                 for c in range(3):
                     out[c, p, here, :] = E[c, p, here, :] + R[c, p // 2, here, :]
+
+        @pl.when(has_far)
+        def _():
+            f_far(k).wait_recv()
+
+        for i in range(part // 8):
+            outer_sweep(out, p_far, q_far, pl.multiple_of(y + i * 8, 8))
 
     for copy in near1 + [f_near, c_near]:
         copy.wait_send()

time: 19.7 us -> 19.4 us (0.985)
  Pallas kernels: 18.7 us -> 18.4 us
    pallas_call x1, Pallas kernels: 18.7 us -> 18.4 us  [per_device(): pl.pallas_call(functools.partial(kernel, tiles), out_shape=jax.ShapeDtype...]
where the time goes in v5:
time: 19.4 us; the launch traced here: 19.3 us
  Pallas kernels  18.4 us (95%)
  local copies, waits for them, and re-layouts  0.88 us (5%)
    pallas_call x1, Pallas kernels, per_device(): pl.pallas_call(functools.partial(kernel, tiles), out_shape=jax.ShapeDtype...  18.4 us
    unnamed x1, local copies, waits for them, and re-layouts  0.88 us

profile of v5, /device:TPU:3, one launch (start us, length us, event | category | flops | bytes accessed | tf_op | source)
XLA Modules:
  0.0 19.3 jit_solution(12256734004387280849)
XLA Ops:
  0.0 18.4 %shard_map.46 = f32[3,4,128,128]{3,2,1,0:T(8,128)S(1)} custom-call(f32[3,4,128,128]{3,2,1,0:T(8,128)} %load_hbm.1, f32[3,4,128,128]{3,2,1,0:T(8,128)} %u_hbm.1, s32[4,128,128]{2,1,0:T(8,128)} %lab_hbm.1, s32[4,128,128]{2,1,0:T(8,128)} %dam_hbm.1), custom_call_target="tpu_custom_call" | custom-call | tf_op jit(solution)/shard_map/pallas_call | solution.py:554
  18.4 0.9 %copy.6 = f32[3,4,128,128]{3,2,1,0:T(8,128)} copy(f32[3,4,128,128]{3,2,1,0:T(8,128)S(1)} %shard_map.46) | data formatting | bytes 1572864

commit v6 on v5

--- a/solution.py
+++ b/solution.py
@@ -52,8 +52,9 @@
     return half * degrade, normal * degrade
 
 
-def kernel(tiles, load_hbm, u_hbm, lab_hbm, dam_hbm, out, U, F, L, INV, R, E, H, K, LAB, DAM, S1, S1R, S2, S2R,
+def kernel(tiles, load_hbm, u_hbm, lab_hbm, dam_hbm, out, U, F, L, INV, R, E, H, K, CODE, S1, S1R, S2, S2R,
            PN, QN, PF, QF, W2, F2, I2, W3, F3, I3, EX, local_sem, send_sem, recv_sem):
+    LAB, DAM = CODE.at[0], CODE.at[1]
     me = lax.axis_index("tile")
     sec = lax.axis_index("sec")
     odd = lax.rem(me, 2)
@@ -79,7 +80,7 @@
         pltpu.make_async_copy(u_hbm, U.at[:, pl.ds(1, X), pl.ds(OFF, Y)], local_sem.at[2]),
         pltpu.make_async_copy(load_hbm, L, local_sem.at[3]),
     ]
-    for copy in loads:
+    for copy in loads[:3]:
         copy.start()
 
     own_row = jnp.where(sec == 0, OFF + Y - 1, OFF)
@@ -116,8 +117,7 @@
         y = part_of(k)
         here, there = pl.ds(y, part), pl.ds(OFF + y, part)
         return [
-            remote(LAB.at[p_far, here], LAB.at[X + 1 - q_far, here], 3 * k, far),
-            remote(DAM.at[p_far, here], DAM.at[X + 1 - q_far, here], 3 * k + 1, far),
+            remote(CODE.at[:, p_far, here], CODE.at[:, X + 1 - q_far, here], 3 * k, far),
             remote(U.at[:, p_far, there], U.at[:, X + 1 - q_far, there], 3 * k + 2, far),
         ]
 
@@ -129,8 +129,7 @@
         return remote(PF.at[k], QF.at[k], 4 * PARTS + k, far)
 
     near1 = [
-        remote(LAB.at[p_near], LAB.at[X + 1 - q_near], base, near),
-        remote(DAM.at[p_near], DAM.at[X + 1 - q_near], base + 1, near),
+        remote(CODE.at[:, p_near], CODE.at[:, X + 1 - q_near], base, near),
         remote(U.at[:, p_near, rows], U.at[:, X + 1 - q_near, rows], base + 2, near),
     ]
     cross1 = remote(S1, S1R, base + 3, across)
@@ -144,6 +143,8 @@
 
     for copy in near1:
         copy.start()
+
+    loads[3].start()
 
     @pl.loop(0, Y // 8)
     def _(i):
@@ -344,6 +345,11 @@
     half = part2 // 2
     odd_half = odd2[:half]
 
+    deep_pieces = [
+        (0, part3 // 2, [(0, 0), (0, part3 // 2), (1, 0), (1, part3 // 2)]),
+        (part3 // 2, part3 // 4, [(2, n * (part3 // 4)) for n in range(4)]),
+    ]
+
     def packed(V, c, p, y2):
         return jnp.where(odd_half, V[c, p, pl.ds(OFF + y2 + half, half), :], V[c, p, pl.ds(OFF + y2, half), :])
 
@@ -406,7 +412,6 @@
         for m, M in enumerate((H, K)):
             W2[m, 2 * odd, at2, :] = x_face(M, p_far, q_far, y)
             W3[m, odd, at3, :] = quads(coarse_rows(m, 2 * odd, y2, 0) + coarse_rows(m, 2 * odd, y2, 1))
-        deep = jnp.zeros(shape3, jnp.float32)
         for c in range(3):
             kx = kinds(c)[0]
             inv = relaxation / (I2[c, j_far, at2, :] + W2[kx, 2 * odd, at2, :])
@@ -420,11 +425,16 @@
             res = res + EX[c, 1, pl.ds(y2, part3, stride=2), :] + EX[c, 1, pl.ds(y2 + 1, part3, stride=2), :]
             first = quads(res) * inv
             F3[c, 1, pl.ds(OFF + y3, part3), :] = first
-            deep = jnp.where(quad == c, first, deep)
             PF[k, pl.ds(half * c, half), :] = packed(F2, c, 1 + j_far, y2)
             PN[k, pl.ds(half * c, half), :] = packed(F2, c, 1 + j_near, y2)
-        PF[k, pl.ds(3 * half, part3), :] = deep
-        PN[k, pl.ds(3 * half, part3), :] = deep
+        for first_row, count, pieces in deep_pieces:
+            quad_now = quad[:count]
+            deep = F3[pieces[0][0], 1, pl.ds(OFF + y3 + pieces[0][1], count), :]
+            for slot in range(1, 4):
+                c, row = pieces[slot]
+                deep = jnp.where(quad_now == slot, F3[c, 1, pl.ds(OFF + y3 + row, count), :], deep)
+            PF[k, pl.ds(3 * half + first_row, count), :] = deep
+            PN[k, pl.ds(3 * half + first_row, count), :] = deep
 
         @pl.when(has_far)
         def _():
@@ -477,11 +487,12 @@
                 v = jnp.where(present, v, 0.0)
             F2[c, q2, pl.ds(OFF + y2, half), :] = jnp.where(odd_half, roll(v, 1), v)
             F2[c, q2, pl.ds(OFF + y2 + half, half), :] = jnp.where(odd_half, v, roll(v, -1))
-        v = Q[k, pl.ds(3 * half, part3), :]
-        if present is not None:
-            v = jnp.where(present, v, 0.0)
-        for c in range(3):
-            F3[c, q3, pl.ds(OFF + y3, part3), :] = spread_quad(v, c, quad)
+        for first_row, count, pieces in deep_pieces:
+            v = Q[k, pl.ds(3 * half + first_row, count), :]
+            if present is not None:
+                v = jnp.where(present, v, 0.0)
+            for slot, (c, row) in enumerate(pieces):
+                F3[c, q3, pl.ds(OFF + y3 + row, count), :] = spread_quad(v, slot, quad[:count])
 
     c_near.wait_recv()
     for k in range(PARTS):
@@ -565,16 +576,15 @@
             pltpu.VMEM((3, X, Y, Z), f32),
             pltpu.VMEM((X + 2, padded, Z), f32),
             pltpu.VMEM((X + 2, padded, Z), f32),
-            pltpu.VMEM((X + 2, Y, Z), i32),
-            pltpu.VMEM((X + 2, Y, Z), i32),
+            pltpu.VMEM((2, X + 2, Y, Z), i32),
             pltpu.VMEM((20, Z), f32),
             pltpu.VMEM((20, Z), f32),
             pltpu.VMEM((16, Z), f32),
             pltpu.VMEM((16, Z), f32),
-            pltpu.VMEM((PARTS, Y // PARTS, Z), f32),
-            pltpu.VMEM((PARTS, Y // PARTS, Z), f32),
-            pltpu.VMEM((PARTS, Y // PARTS, Z), f32),
-            pltpu.VMEM((PARTS, Y // PARTS, Z), f32),
+            pltpu.VMEM((PARTS, Y * 15 // (16 * PARTS), Z), f32),
+            pltpu.VMEM((PARTS, Y * 15 // (16 * PARTS), Z), f32),
+            pltpu.VMEM((PARTS, Y * 15 // (16 * PARTS), Z), f32),
+            pltpu.VMEM((PARTS, Y * 15 // (16 * PARTS), Z), f32),
             pltpu.VMEM((2, 11, Y // 2, Z), f32),
             pltpu.VMEM((3, 4, Y // 2 + 2 * OFF, Z), f32),
             pltpu.VMEM((3, 2, Y // 2, Z), f32),

time: 19.4 us -> 19.3 us (level)
  no operation moved by 1% of the time
where the time goes in v6:
time: 19.3 us; the launch traced here: 19.2 us
  Pallas kernels  18.3 us (95%)
  local copies, waits for them, and re-layouts  0.88 us (5%)
    pallas_call x1, Pallas kernels, per_device(): pl.pallas_call(functools.partial(kernel, tiles), out_shape=jax.ShapeDtype...  18.3 us
    unnamed x1, local copies, waits for them, and re-layouts  0.88 us

profile of v6, /device:TPU:3, one launch (start us, length us, event | category | flops | bytes accessed | tf_op | source)
XLA Modules:
  0.0 19.2 jit_solution(12203013887294686568)
XLA Ops:
  0.0 18.3 %shard_map.46 = f32[3,4,128,128]{3,2,1,0:T(8,128)S(1)} custom-call(f32[3,4,128,128]{3,2,1,0:T(8,128)} %load_hbm.1, f32[3,4,128,128]{3,2,1,0:T(8,128)} %u_hbm.1, s32[4,128,128]{2,1,0:T(8,128)} %lab_hbm.1, s32[4,128,128]{2,1,0:T(8,128)} %dam_hbm.1), custom_call_target="tpu_custom_call" | custom-call | tf_op jit(solution)/shard_map/pallas_call | solution.py:565
  18.3 0.9 %copy.6 = f32[3,4,128,128]{3,2,1,0:T(8,128)} copy(f32[3,4,128,128]{3,2,1,0:T(8,128)S(1)} %shard_map.46) | data formatting | bytes 1572864

commit v7 on v6

--- a/solution.py
+++ b/solution.py
@@ -52,9 +52,10 @@
     return half * degrade, normal * degrade
 
 
-def kernel(tiles, load_hbm, u_hbm, lab_hbm, dam_hbm, out, U, F, L, INV, R, E, H, K, CODE, S1, S1R, S2, S2R,
+def kernel(tiles, load_hbm, u_hbm, lab_hbm, dam_hbm, out, U, F, L, INV, R, E, CODE, S1, S1R, S2, S2R,
            PN, QN, PF, QF, W2, F2, I2, W3, F3, I3, EX, local_sem, send_sem, recv_sem):
     LAB, DAM = CODE.at[0], CODE.at[1]
+    H, K = U.at[3], U.at[4]
     me = lax.axis_index("tile")
     sec = lax.axis_index("sec")
     odd = lax.rem(me, 2)
@@ -77,7 +78,7 @@
     loads = [
         pltpu.make_async_copy(lab_hbm, LAB.at[pl.ds(1, X)], local_sem.at[0]),
         pltpu.make_async_copy(dam_hbm, DAM.at[pl.ds(1, X)], local_sem.at[1]),
-        pltpu.make_async_copy(u_hbm, U.at[:, pl.ds(1, X), pl.ds(OFF, Y)], local_sem.at[2]),
+        pltpu.make_async_copy(u_hbm, U.at[pl.ds(0, 3), pl.ds(1, X), pl.ds(OFF, Y)], local_sem.at[2]),
         pltpu.make_async_copy(load_hbm, L, local_sem.at[3]),
     ]
     for copy in loads[:3]:
@@ -94,6 +95,17 @@
         h, k = moduli(LAB[1 + p, pl.ds(own_row - OFF, 1), :], DAM[1 + p, pl.ds(own_row - OFF, 1), :])
         S1[pl.ds(p, 1), :] = h
         S1[pl.ds(X + p, 1), :] = k
+
+    def own_moduli(planes):
+        @pl.loop(0, Y // 8)
+        def _(i):
+            y = pl.multiple_of(i * 8, 8)
+            for p in planes:
+                h, k = moduli(LAB[p, pl.ds(y, 8), :], DAM[p, pl.ds(y, 8), :])
+                H[p, pl.ds(OFF + y, 8), :] = h
+                K[p, pl.ds(OFF + y, 8), :] = k
+
+    own_moduli((1, X))
     loads[2].wait()
     for f in range(2, 5):
         for p in range(X):
@@ -117,7 +129,6 @@
         y = part_of(k)
         here, there = pl.ds(y, part), pl.ds(OFF + y, part)
         return [
-            remote(CODE.at[:, p_far, here], CODE.at[:, X + 1 - q_far, here], 3 * k, far),
             remote(U.at[:, p_far, there], U.at[:, X + 1 - q_far, there], 3 * k + 2, far),
         ]
 
@@ -129,7 +140,6 @@
         return remote(PF.at[k], QF.at[k], 4 * PARTS + k, far)
 
     near1 = [
-        remote(CODE.at[:, p_near], CODE.at[:, X + 1 - q_near], base, near),
         remote(U.at[:, p_near, rows], U.at[:, X + 1 - q_near, rows], base + 2, near),
     ]
     cross1 = remote(S1, S1R, base + 3, across)
@@ -146,14 +156,7 @@
 
     loads[3].start()
 
-    @pl.loop(0, Y // 8)
-    def _(i):
-        y = pl.multiple_of(i * 8, 8)
-        for p in range(1, X + 1):
-            h, k = moduli(LAB[p, pl.ds(y, 8), :], DAM[p, pl.ds(y, 8), :])
-            H[p, pl.ds(OFF + y, 8), :] = h
-            K[p, pl.ds(OFF + y, 8), :] = k
-
+    own_moduli(range(2, X))
     for ref in faces:
         for p in range(X):
             ref[p, pl.ds(edge_row, 1), :] = zero_row
@@ -236,12 +239,7 @@
 
     def outer_face(p, q, y, present):
         here, there = pl.ds(y, 8), pl.ds(OFF + y, 8)
-        h, k = moduli(LAB[q, here, :], DAM[q, here, :])
-        if present is not None:
-            h = jnp.where(present, h, 0.0)
-            k = jnp.where(present, k, 0.0)
-        H[q, there, :] = h
-        K[q, there, :] = k
+        h, k = H[q, there, :], K[q, there, :]
         s = h + H[p, there, :]
         t = k + K[p, there, :]
         j = (p - 1) // 2
@@ -568,14 +566,12 @@
         in_specs=[pl.BlockSpec(memory_space=pltpu.HBM)] * 4,
         out_specs=pl.BlockSpec(memory_space=pltpu.VMEM),
         scratch_shapes=[
-            pltpu.VMEM((3, X + 2, padded, Z), f32),
+            pltpu.VMEM((5, X + 2, padded, Z), f32),
             pltpu.VMEM((3, X + 2, padded, Z), f32),
             pltpu.VMEM((3, X, Y, Z), f32),
             pltpu.VMEM((3, X, Y, Z), f32),
             pltpu.VMEM((3, X // 2, Y, Z), f32),
             pltpu.VMEM((3, X, Y, Z), f32),
-            pltpu.VMEM((X + 2, padded, Z), f32),
-            pltpu.VMEM((X + 2, padded, Z), f32),
             pltpu.VMEM((2, X + 2, Y, Z), i32),
             pltpu.VMEM((20, Z), f32),
             pltpu.VMEM((20, Z), f32),

time: 19.3 us -> 19.4 us (level)
  no operation moved by 1% of the time
where the time goes in v7:
time: 19.4 us; the launch traced here: 19.2 us
  Pallas kernels  18.3 us (94%)
  local copies, waits for them, and re-layouts  0.88 us (5%)
    pallas_call x1, Pallas kernels, per_device(): pl.pallas_call(functools.partial(kernel, tiles), out_shape=jax.ShapeDtype...  18.3 us
    unnamed x1, local copies, waits for them, and re-layouts  0.88 us

profile of v7, /device:TPU:3, one launch (start us, length us, event | category | flops | bytes accessed | tf_op | source)
XLA Modules:
  0.0 19.2 jit_solution(5127315476781520964)
XLA Ops:
  0.0 18.3 %shard_map.46 = f32[3,4,128,128]{3,2,1,0:T(8,128)S(1)} custom-call(f32[3,4,128,128]{3,2,1,0:T(8,128)} %load_hbm.1, f32[3,4,128,128]{3,2,1,0:T(8,128)} %u_hbm.1, s32[4,128,128]{2,1,0:T(8,128)} %lab_hbm.1, s32[4,128,128]{2,1,0:T(8,128)} %dam_hbm.1), custom_call_target="tpu_custom_call" | custom-call | tf_op jit(solution)/shard_map/pallas_call | solution.py:563
  18.3 0.9 %copy.6 = f32[3,4,128,128]{3,2,1,0:T(8,128)} copy(f32[3,4,128,128]{3,2,1,0:T(8,128)S(1)} %shard_map.46) | data formatting | bytes 1572864

commit v8 on v7

--- a/solution.py
+++ b/solution.py
@@ -434,15 +434,15 @@
             PF[k, pl.ds(3 * half + first_row, count), :] = deep
             PN[k, pl.ds(3 * half + first_row, count), :] = deep
 
+        @pl.when(k == 0)
+        def _():
+            pack_rows()
+            cross2.start()
+
         @pl.when(has_far)
         def _():
             c_far(k).start()
             f_far(k).start()
-
-        @pl.when(k == 0)
-        def _():
-            pack_rows()
-            cross2.start()
 
     c_near = remote(PN, QN, base + 6, near)
     c_near.start()

time: 19.4 us -> 19.4 us (level)
  no operation moved by 1% of the time
where the time goes in v8:
time: 19.4 us; the launch traced here: 19.2 us
  Pallas kernels  18.3 us (94%)
  local copies, waits for them, and re-layouts  0.88 us (5%)
    pallas_call x1, Pallas kernels, per_device(): pl.pallas_call(functools.partial(kernel, tiles), out_shape=jax.ShapeDtype...  18.3 us
    unnamed x1, local copies, waits for them, and re-layouts  0.88 us

profile of v8, /device:TPU:3, one launch (start us, length us, event | category | flops | bytes accessed | tf_op | source)
XLA Modules:
  0.0 19.2 jit_solution(4924171511624474238)
XLA Ops:
  0.0 18.3 %shard_map.46 = f32[3,4,128,128]{3,2,1,0:T(8,128)S(1)} custom-call(f32[3,4,128,128]{3,2,1,0:T(8,128)} %load_hbm.1, f32[3,4,128,128]{3,2,1,0:T(8,128)} %u_hbm.1, s32[4,128,128]{2,1,0:T(8,128)} %lab_hbm.1, s32[4,128,128]{2,1,0:T(8,128)} %dam_hbm.1), custom_call_target="tpu_custom_call" | custom-call | tf_op jit(solution)/shard_map/pallas_call | solution.py:563
  18.3 0.9 %copy.6 = f32[3,4,128,128]{3,2,1,0:T(8,128)} copy(f32[3,4,128,128]{3,2,1,0:T(8,128)S(1)} %shard_map.46) | data formatting | bytes 1572864

commit v9 on v6

--- a/solution.py
+++ b/solution.py
@@ -436,15 +436,15 @@
             PF[k, pl.ds(3 * half + first_row, count), :] = deep
             PN[k, pl.ds(3 * half + first_row, count), :] = deep
 
+        @pl.when(k == 0)
+        def _():
+            pack_rows()
+            cross2.start()
+
         @pl.when(has_far)
         def _():
             c_far(k).start()
             f_far(k).start()
-
-        @pl.when(k == 0)
-        def _():
-            pack_rows()
-            cross2.start()
 
     c_near = remote(PN, QN, base + 6, near)
     c_near.start()

time: 19.3 us -> 19.3 us (level)
  no operation moved by 1% of the time
where the time goes in v9:
time: 19.3 us; the launch traced here: 19.2 us
  Pallas kernels  18.3 us (95%)
  local copies, waits for them, and re-layouts  0.88 us (5%)
    pallas_call x1, Pallas kernels, per_device(): pl.pallas_call(functools.partial(kernel, tiles), out_shape=jax.ShapeDtype...  18.3 us
    unnamed x1, local copies, waits for them, and re-layouts  0.88 us

profile of v9, /device:TPU:3, one launch (start us, length us, event | category | flops | bytes accessed | tf_op | source)
XLA Modules:
  0.0 19.2 jit_solution(8506801632139810529)
XLA Ops:
  0.0 18.3 %shard_map.46 = f32[3,4,128,128]{3,2,1,0:T(8,128)S(1)} custom-call(f32[3,4,128,128]{3,2,1,0:T(8,128)} %load_hbm.1, f32[3,4,128,128]{3,2,1,0:T(8,128)} %u_hbm.1, s32[4,128,128]{2,1,0:T(8,128)} %lab_hbm.1, s32[4,128,128]{2,1,0:T(8,128)} %dam_hbm.1), custom_call_target="tpu_custom_call" | custom-call | tf_op jit(solution)/shard_map/pallas_call | solution.py:565
  18.3 0.9 %copy.6 = f32[3,4,128,128]{3,2,1,0:T(8,128)} copy(f32[3,4,128,128]{3,2,1,0:T(8,128)S(1)} %shard_map.46) | data formatting | bytes 1572864
